TPU v7x, 32 devices: a whole 2x2x4 slice. The times are simulated.
32 devices in a mesh: dp: 8 (over y, x, core), seq: 4 (over z).
Axes of the slice: x: 2, y: 2, z: 4, core: 2. Of those that a mesh axis runs over, the one named last changes fastest.
Arguments:
- tokens: bfloat16 [16, 1024, 1280], P('dp', 'seq'), may hold values from -6 to 6
- lengths: int32 [16], P('dp'), may hold values from 204 to 1024, as said below
- cotangent: bfloat16 [16, 1024, 1280], P('dp', 'seq'), may hold values from -6 to 6
- w_qkv: bfloat16 [1280, 3840], P(('dp', 'seq')), may hold values from -0.15625 to 0.15625
- w_out: bfloat16 [1280, 1280], P(('dp', 'seq')), may hold values from -2.5 to 2.5
- w_up: bfloat16 [1280, 5120], P(('dp', 'seq')), may hold values from -0.15625 to 0.15625
- w_down: bfloat16 [5120, 1280], P(('dp', 'seq')), may hold values from -0.078125 to 0.078125
- gain_one: bfloat16 [1280], P(('dp', 'seq')), may hold values from 0.099609375 to 1.8984375
- shift_one: bfloat16 [1280], P(('dp', 'seq')), may hold values from -3 to 3
- bias_query: bfloat16 [1280], P(('dp', 'seq')), may hold values from -3 to 3
- bias_value: bfloat16 [1280], P(('dp', 'seq')), may hold values from -3 to 3
- bias_out: bfloat16 [1280], P(('dp', 'seq')), may hold values from -3 to 3
- gain_two: bfloat16 [1280], P(('dp', 'seq')), may hold values from 0.099609375 to 1.8984375
- shift_two: bfloat16 [1280], P(('dp', 'seq')), may hold values from -3 to 3
- bias_up: bfloat16 [5120], P(('dp', 'seq')), may hold values from -3 to 3
- bias_down: bfloat16 [1280], P(('dp', 'seq')), may hold values from -3 to 3
Outputs:
- output: bfloat16 [16, 1024, 1280], P('dp', 'seq')
- input_grad: float32 [16, 1024, 1280], P('dp', 'seq')
- grad_qkv: float32 [1280, 3840], P(('dp', 'seq'))
- grad_out: float32 [1280, 1280], P(('dp', 'seq'))
- grad_up: float32 [1280, 5120], P(('dp', 'seq'))
- grad_down: float32 [5120, 1280], P(('dp', 'seq'))
- grad_gain_one: float32 [1280], P(('dp', 'seq'))
- grad_shift_one: float32 [1280], P(('dp', 'seq'))
- grad_bias_query: float32 [1280], P(('dp', 'seq'))
- grad_bias_value: float32 [1280], P(('dp', 'seq'))
- grad_bias_out: float32 [1280], P(('dp', 'seq'))
- grad_gain_two: float32 [1280], P(('dp', 'seq'))
- grad_shift_two: float32 [1280], P(('dp', 'seq'))
- grad_bias_up: float32 [5120], P(('dp', 'seq'))
- grad_bias_down: float32 [1280], P(('dp', 'seq'))
Inputs may be any that keep to these rules, and one draw needn't show every extreme that they name: Cell c holds genes at positions 0 to lengths[c]-1; the rest up to 1024 is padding that is masked as keys. Some cell has all 1024 positions.
All inputs are finite; a program needn't handle non-finite values.
Results may differ from a plain program's by a relative error of at most 0.03.
Values may be sent and summed in bfloat16 or wider, within the bound.
No kernel may reach another device: no remote copies, remote signals or barrier semaphores. Data moves between devices by JAX's collectives and lax.ppermute only.
A program may use at most 224 MiB of HBM per device.

v0:
```python
import jax
import jax.numpy as jnp
from jax import lax
from jax.sharding import PartitionSpec as P

HEADS = 20
MICRO = 2


EPSILON = 1e-05


def layer_norm(values, gain, shift):
    row_mean = jnp.mean(values, axis=-1, keepdims=True)
    centered = values - row_mean
    variance = jnp.mean(centered * centered, axis=-1, keepdims=True)
    return centered * lax.rsqrt(variance + EPSILON) * gain + shift


def gelu_exact(values):
    return jax.nn.gelu(values, approximate=False)


def flatten(values):
    return values.reshape(-1, values.shape[-1])


def contract_rows(left, right):
    return lax.dot_general(
        left, right, (((0,), (0,)), ((), ())), preferred_element_type=jnp.float32
    )


def times_transpose(left, right):
    return lax.dot_general(
        left, right, (((1,), (1,)), ((), ())), preferred_element_type=jnp.float32
    )


def split_heads(values):
    return values.reshape(values.shape[0], values.shape[1], HEADS, values.shape[2] // HEADS)


def masked_scores(queries, keys_all, counts, first_key):
    scale = (queries.shape[-1] // HEADS) ** (-0.5)
    scores = (
        jnp.einsum(
            "pqhe,pkhe->phqk",
            split_heads(queries),
            split_heads(keys_all),
            preferred_element_type=jnp.float32,
        )
        * scale
    )
    positions = first_key + jnp.arange(keys_all.shape[1])
    valid = positions[None, :] < counts[:, None]
    return jnp.where(valid[:, None, None, :], scores, -1000000000.0)


def forward_micro(weights, inputs, counts):
    (
        w_qkv,
        w_out,
        w_up,
        w_down,
        gain_one,
        shift_one,
        bias_query,
        bias_value,
        bias_out,
        gain_two,
        shift_two,
        bias_up,
        bias_down,
    ) = weights
    width = inputs.shape[2]
    normed, pull_one = jax.vjp(
        layer_norm, inputs, gain_one.astype(jnp.float32), shift_one.astype(jnp.float32)
    )
    normed_low = normed.astype(jnp.bfloat16)
    project = jnp.dot(flatten(normed_low), w_qkv, preferred_element_type=jnp.float32)
    project = project.reshape(inputs.shape[0], inputs.shape[1], 3 * width)
    queries = (project[..., :width] + bias_query).astype(jnp.bfloat16)
    key_local = project[..., width : 2 * width].astype(jnp.bfloat16)
    value_local = (project[..., 2 * width :] + bias_value).astype(jnp.bfloat16)
    keys_all, values_all = (
        lax.all_gather(key_local, "seq", axis=1, tiled=True),
        lax.all_gather(value_local, "seq", axis=1, tiled=True),
    )
    scores = masked_scores(queries, keys_all, counts, 0)
    row_max = jnp.max(scores, axis=-1, keepdims=True)
    exponent = jnp.exp(scores - row_max)
    row_sum = jnp.sum(exponent, axis=-1, keepdims=True)
    soft_low = (exponent / row_sum).astype(jnp.bfloat16)
    mixed = jnp.einsum(
        "phqk,pkhe->pqhe", soft_low, split_heads(values_all), preferred_element_type=jnp.float32
    )
    mixed_low = mixed.reshape(inputs.shape).astype(jnp.bfloat16)
    attended = (
        jnp.dot(flatten(mixed_low), w_out, preferred_element_type=jnp.float32).reshape(inputs.shape)
        + bias_out
    )
    middle = inputs + attended
    normed_two, pull_two = jax.vjp(
        layer_norm, middle, gain_two.astype(jnp.float32), shift_two.astype(jnp.float32)
    )
    second_low = flatten(normed_two.astype(jnp.bfloat16))
    hidden = jnp.dot(second_low, w_up, preferred_element_type=jnp.float32) + bias_up
    active, pull_gelu = jax.vjp(gelu_exact, hidden)
    active_low = active.astype(jnp.bfloat16)
    branch = (
        jnp.dot(active_low, w_down, preferred_element_type=jnp.float32).reshape(inputs.shape)
        + bias_down
    )
    output = (middle + branch).astype(jnp.bfloat16)
    saved_residual = {
        "pull_one": pull_one,
        "normed_low": normed_low,
        "queries": queries,
        "key_local": key_local,
        "value_local": value_local,
        "keys_all": keys_all,
        "values_all": values_all,
        "row_max": row_max,
        "row_sum": row_sum,
        "mixed_low": mixed_low,
        "pull_two": pull_two,
        "second_low": second_low,
        "pull_gelu": pull_gelu,
        "active_low": active_low,
        "counts": counts,
    }
    return (output, saved_residual)


def backward_micro(weights, saved_residual, incoming):
    (
        w_qkv,
        w_out,
        w_up,
        w_down,
        gain_one,
        shift_one,
        bias_query,
        bias_value,
        bias_out,
        gain_two,
        shift_two,
        bias_up,
        bias_down,
    ) = weights
    shape = incoming.shape
    width = shape[2]
    d_output = incoming.astype(jnp.float32)
    d_branch = flatten(incoming)
    grad_bias_down = jnp.sum(d_branch.astype(jnp.float32), axis=0)
    grad_down = contract_rows(saved_residual["active_low"], d_branch)
    d_active = times_transpose(d_branch, w_down)
    d_hidden = saved_residual["pull_gelu"](d_active)[0].astype(jnp.bfloat16)
    grad_bias_up = jnp.sum(d_hidden.astype(jnp.float32), axis=0)
    grad_up = contract_rows(saved_residual["second_low"], d_hidden)
    d_second = times_transpose(d_hidden, w_up).reshape(shape)
    d_middle_norm, grad_gain_two, grad_shift_two = saved_residual["pull_two"](d_second)
    d_middle = d_output + d_middle_norm
    d_attend = flatten(d_middle).astype(jnp.bfloat16)
    grad_bias_out = jnp.sum(d_attend.astype(jnp.float32), axis=0)
    grad_out = contract_rows(flatten(saved_residual["mixed_low"]), d_attend)
    d_mixed = times_transpose(d_attend, w_out).reshape(shape).astype(jnp.bfloat16)
    keys_all, values_all = (saved_residual["keys_all"], saved_residual["values_all"])
    queries = saved_residual["queries"]
    counts = saved_residual["counts"]
    scale = (width // HEADS) ** (-0.5)
    scores = masked_scores(queries, keys_all, counts, 0)
    soft = jnp.exp(scores - saved_residual["row_max"]) / saved_residual["row_sum"]
    d_mixed_heads = split_heads(d_mixed)
    d_soft = jnp.einsum(
        "pqhe,pkhe->phqk",
        d_mixed_heads,
        split_heads(values_all),
        preferred_element_type=jnp.float32,
    )
    inner = jnp.sum(soft * d_soft, axis=-1, keepdims=True)
    d_scores = (soft * (d_soft - inner)).astype(jnp.bfloat16)
    d_queries = (
        jnp.einsum(
            "phqk,pkhe->pqhe", d_scores, split_heads(keys_all), preferred_element_type=jnp.float32
        )
        * scale
    )
    rows_local = shape[1]
    queries_all, d_mixed_all, max_all, sum_all, inner_all = (
        lax.all_gather(queries, "seq", axis=1, tiled=True),
        lax.all_gather(d_mixed, "seq", axis=1, tiled=True),
        lax.all_gather(
            saved_residual["row_max"][..., 0].astype(jnp.bfloat16), "seq", axis=2, tiled=True
        ).astype(jnp.float32),
        lax.all_gather(
            saved_residual["row_sum"][..., 0].astype(jnp.bfloat16), "seq", axis=2, tiled=True
        ).astype(jnp.float32),
        lax.all_gather(inner[..., 0].astype(jnp.bfloat16), "seq", axis=2, tiled=True).astype(
            jnp.float32
        ),
    )
    first_key = lax.axis_index("seq") * rows_local
    own_scores = masked_scores(queries_all, saved_residual["key_local"], counts, first_key)
    own_soft = jnp.exp(own_scores - max_all[..., None]) / sum_all[..., None]
    own_soft_low = own_soft.astype(jnp.bfloat16)
    d_mixed_all_heads = split_heads(d_mixed_all)
    own_d_soft = jnp.einsum(
        "pqhe,pkhe->phqk",
        d_mixed_all_heads,
        split_heads(saved_residual["value_local"]),
        preferred_element_type=jnp.float32,
    )
    own_d_scores = (own_soft * (own_d_soft - inner_all[..., None])).astype(jnp.bfloat16)
    d_keys = (
        jnp.einsum(
            "phqk,pqhe->pkhe",
            own_d_scores,
            split_heads(queries_all),
            preferred_element_type=jnp.float32,
        )
        * scale
    ).reshape(shape)
    d_values = jnp.einsum(
        "phqk,pqhe->pkhe", own_soft_low, d_mixed_all_heads, preferred_element_type=jnp.float32
    ).reshape(shape)
    d_project = jnp.concatenate([d_queries.reshape(shape), d_keys, d_values], axis=-1).astype(
        jnp.bfloat16
    )
    flat_project = flatten(d_project)
    grad_bias_query = jnp.sum(flat_project[:, :width].astype(jnp.float32), axis=0)
    grad_bias_value = jnp.sum(flat_project[:, 2 * width :].astype(jnp.float32), axis=0)
    grad_qkv = contract_rows(flatten(saved_residual["normed_low"]), flat_project)
    d_normed = times_transpose(flat_project, w_qkv).reshape(shape)
    d_input_norm, grad_gain_one, grad_shift_one = saved_residual["pull_one"](d_normed)
    input_grad = d_middle + d_input_norm
    grads = (
        grad_qkv,
        grad_out,
        grad_up,
        grad_down,
        grad_gain_one,
        grad_shift_one,
        grad_bias_query,
        grad_bias_value,
        grad_bias_out,
        grad_gain_two,
        grad_shift_two,
        grad_bias_up,
        grad_bias_down,
    )
    return (grads, input_grad)


def body(
    tokens,
    lengths,
    cotangent,
    w_qkv,
    w_out,
    w_up,
    w_down,
    gain_one,
    shift_one,
    bias_query,
    bias_value,
    bias_out,
    gain_two,
    shift_two,
    bias_up,
    bias_down,
):
    per_micro_batch = tokens.shape[0] // MICRO
    gathered = (
        lax.all_gather(w_qkv, ("dp", "seq"), axis=0, tiled=True),
        lax.all_gather(w_out, ("dp", "seq"), axis=0, tiled=True),
        lax.all_gather(w_up, ("dp", "seq"), axis=0, tiled=True),
        lax.all_gather(w_down, ("dp", "seq"), axis=0, tiled=True),
        lax.all_gather(gain_one, ("dp", "seq"), axis=0, tiled=True),
        lax.all_gather(shift_one, ("dp", "seq"), axis=0, tiled=True),
        lax.all_gather(bias_query, ("dp", "seq"), axis=0, tiled=True),
        lax.all_gather(bias_value, ("dp", "seq"), axis=0, tiled=True),
        lax.all_gather(bias_out, ("dp", "seq"), axis=0, tiled=True),
        lax.all_gather(gain_two, ("dp", "seq"), axis=0, tiled=True),
        lax.all_gather(shift_two, ("dp", "seq"), axis=0, tiled=True),
        lax.all_gather(bias_up, ("dp", "seq"), axis=0, tiled=True),
        lax.all_gather(bias_down, ("dp", "seq"), axis=0, tiled=True),
    )
    outputs = []
    saved_residuals = []
    for micro_batch_cells in range(MICRO):
        lower_precision = micro_batch_cells * per_micro_batch
        result, saved_residual = forward_micro(
            gathered,
            tokens[lower_precision : lower_precision + per_micro_batch].astype(jnp.float32),
            lengths[lower_precision : lower_precision + per_micro_batch],
        )
        outputs.append(result)
        saved_residuals.append(saved_residual)
    backing_buffer = (
        lax.all_gather(w_qkv, ("dp", "seq"), axis=0, tiled=True),
        lax.all_gather(w_out, ("dp", "seq"), axis=0, tiled=True),
        lax.all_gather(w_up, ("dp", "seq"), axis=0, tiled=True),
        lax.all_gather(w_down, ("dp", "seq"), axis=0, tiled=True),
        lax.all_gather(gain_one, ("dp", "seq"), axis=0, tiled=True),
        lax.all_gather(shift_one, ("dp", "seq"), axis=0, tiled=True),
        lax.all_gather(bias_query, ("dp", "seq"), axis=0, tiled=True),
        lax.all_gather(bias_value, ("dp", "seq"), axis=0, tiled=True),
        lax.all_gather(bias_out, ("dp", "seq"), axis=0, tiled=True),
        lax.all_gather(gain_two, ("dp", "seq"), axis=0, tiled=True),
        lax.all_gather(shift_two, ("dp", "seq"), axis=0, tiled=True),
        lax.all_gather(bias_up, ("dp", "seq"), axis=0, tiled=True),
        lax.all_gather(bias_down, ("dp", "seq"), axis=0, tiled=True),
    )
    totals = tuple((jnp.zeros(member.shape, jnp.float32) for member in backing_buffer))
    input_grads = []
    for micro_batch_cells in range(MICRO):
        lower_precision = micro_batch_cells * per_micro_batch
        grads, input_grad = backward_micro(
            backing_buffer,
            saved_residuals[micro_batch_cells],
            cotangent[lower_precision : lower_precision + per_micro_batch],
        )
        totals = jax.tree.map(jnp.add, totals, grads)
        input_grads.append(input_grad)
    (
        total_qkv,
        total_out,
        total_up,
        total_down,
        total_gain_one,
        total_shift_one,
        total_query,
        total_value,
        total_bias_out,
        total_gain_two,
        summed_second_shift,
        total_bias_up,
        total_bias_down,
    ) = totals
    reduced = (
        lax.psum_scatter(total_qkv, ("dp", "seq"), scatter_dimension=0, tiled=True),
        lax.psum_scatter(total_out, ("dp", "seq"), scatter_dimension=0, tiled=True),
        lax.psum_scatter(total_up, ("dp", "seq"), scatter_dimension=0, tiled=True),
        lax.psum_scatter(total_down, ("dp", "seq"), scatter_dimension=0, tiled=True),
        lax.psum_scatter(total_gain_one, ("dp", "seq"), scatter_dimension=0, tiled=True),
        lax.psum_scatter(total_shift_one, ("dp", "seq"), scatter_dimension=0, tiled=True),
        lax.psum_scatter(total_query, ("dp", "seq"), scatter_dimension=0, tiled=True),
        lax.psum_scatter(total_value, ("dp", "seq"), scatter_dimension=0, tiled=True),
        lax.psum_scatter(total_bias_out, ("dp", "seq"), scatter_dimension=0, tiled=True),
        lax.psum_scatter(total_gain_two, ("dp", "seq"), scatter_dimension=0, tiled=True),
        lax.psum_scatter(summed_second_shift, ("dp", "seq"), scatter_dimension=0, tiled=True),
        lax.psum_scatter(total_bias_up, ("dp", "seq"), scatter_dimension=0, tiled=True),
        lax.psum_scatter(total_bias_down, ("dp", "seq"), scatter_dimension=0, tiled=True),
    )
    output = jnp.concatenate(outputs, axis=0)
    input_grad = jnp.concatenate(input_grads, axis=0)
    return (
        output,
        input_grad,
        reduced[0],
        reduced[1],
        reduced[2],
        reduced[3],
        reduced[4],
        reduced[5],
        reduced[6],
        reduced[7],
        reduced[8],
        reduced[9],
        reduced[10],
        reduced[11],
        reduced[12],
    )


def solution(mesh):
    placed = (
        P("dp", "seq", None),
        P("dp"),
        P("dp", "seq", None),
        P(("dp", "seq"), None),
        P(("dp", "seq"), None),
        P(("dp", "seq"), None),
        P(("dp", "seq"), None),
        P(("dp", "seq")),
        P(("dp", "seq")),
        P(("dp", "seq")),
        P(("dp", "seq")),
        P(("dp", "seq")),
        P(("dp", "seq")),
        P(("dp", "seq")),
        P(("dp", "seq")),
        P(("dp", "seq")),
    )
    return jax.shard_map(
        body,
        mesh=mesh,
        in_specs=placed,
        out_specs=(
            P("dp", "seq", None),
            P("dp", "seq", None),
            P(("dp", "seq"), None),
            P(("dp", "seq"), None),
            P(("dp", "seq"), None),
            P(("dp", "seq"), None),
            P(("dp", "seq")),
            P(("dp", "seq")),
            P(("dp", "seq")),
            P(("dp", "seq")),
            P(("dp", "seq")),
            P(("dp", "seq")),
            P(("dp", "seq")),
            P(("dp", "seq")),
            P(("dp", "seq")),
        ),
        check_vma=False,
    )
```

profile of v0, /device:TPU:0, one launch (start us, length us, event | category | flops | bytes accessed | tf_op | source)
XLA Modules:
  0.0 2376.8 jit_solution(13794883017884974855)
XLA Ops:
  15.6 43.8 %all-reduce.19 = (bf16[1280]{0:T(1024)(128)(2,1)S(1)}, bf16[1280]{0:T(1024)(128)(2,1)S(1)}, bf16[1280]{0:T(1024)(128)(2,1)S(1)}, bf16[1280]{0:T(1024)(128)(2,1)S...) all-reduce(bf16[1280]{0:T(1024)(128)(2,1)S(1)} %dynamic-update-slic, ...), channel_id=1, replica_groups=mesh['dp'=8,'seq'=4] {'dp','seq'}, use_global_device_ids=true, to_apply=%add.1 | all-reduce | flops 15360 | bytes 61440
  62.8 34.0 %all-gather.21.cloned.1.call-done = bf16[1280,3840]{1,0:T(8,128)(2,1)} async-done(((bf16[40,3840]{1,0:T(8,128)(2,1)}), bf16[1280,3840]{1,0:T(8,128)(2,1)}) %all-gather.21.cloned.1.call-update) | async-done | bytes 9830416 | tf_op jit(solution)/shard_map/all_gather | solution.py:276
  138.4 21.5 all-gather.25.cloned.1.call-done
  277.8 51.1 %all-gather.33.cloned.1.call-done = bf16[1,1024,1280]{2,1,0:T(8,128)(2,1)} async-done(((bf16[1,256,1280]{2,1,0:T(8,128)(2,1)}), bf16[1,1024,1280]{2,1,0:T(8,128)(2,1)}) %all-gather.33.cloned.1.call-update) | async-done | bytes 2621456 | tf_op jit(solution)/shard_map/all_gather | solution.py:88
  333.2 50.6 %all-gather.37.cloned.1.call-done = bf16[1,1024,1280]{2,1,0:T(8,128)(2,1)} async-done(((bf16[1,256,1280]{2,1,0:T(8,128)(2,1)}), bf16[1,1024,1280]{2,1,0:T(8,128)(2,1)}) %all-gather.37.cloned.1.call-update) | async-done | bytes 2621456 | tf_op jit(solution)/shard_map/all_gather | solution.py:192
  388.3 51.2 %all-gather.39.cloned.1.call-done = bf16[1,1024,1280]{2,1,0:T(8,128)(2,1)} async-done(((bf16[1,256,1280]{2,1,0:T(8,128)(2,1)}), bf16[1,1024,1280]{2,1,0:T(8,128)(2,1)}) %all-gather.39.cloned.1.call-update) | async-done | bytes 2621456 | tf_op jit(solution)/shard_map/all_gather | solution.py:192
  454.7 46.0 %all-gather.27.cloned.1.call-done = bf16[1280,1280]{1,0:T(8,128)(2,1)} async-done(((bf16[40,1280]{1,0:T(8,128)(2,1)}), bf16[1280,1280]{1,0:T(8,128)(2,1)}) %all-gather.27.cloned.1.call-update) | async-done | bytes 3276816 | tf_op jit(solution)/shard_map/all_gather | solution.py:277
  539.8 60.2 %all-gather.29.cloned.1.call-done = bf16[1280,5120]{1,0:T(8,128)(2,1)} async-done(((bf16[40,5120]{1,0:T(8,128)(2,1)}), bf16[1280,5120]{1,0:T(8,128)(2,1)}) %all-gather.29.cloned.1.call-update) | async-done | bytes 13107216 | tf_op jit(solution)/shard_map/all_gather | solution.py:278
  600.0 20.7 multiply_convert_fusion.9
  620.7 18.2 multiply_convert_fusion.8
  638.9 60.1 %all-gather.31.cloned.1.call-done = bf16[5120,1280]{1,0:T(8,128)(2,1)} async-done(((bf16[160,1280]{1,0:T(8,128)(2,1)}), bf16[5120,1280]{1,0:T(8,128)(2,1)}) %all-gather.31.cloned.1.call-update) | async-done | bytes 13107216 | tf_op jit(solution)/shard_map/all_gather | solution.py:279
  699.0 14.7 convert_reduce_fusion
  724.5 14.6 convert_reduce_fusion.1
  765.2 16.4 multiply_reduce_fusion.1
  788.6 17.4 fusion.78
  807.1 18.2 multiply_reduce_fusion
  853.3 17.2 fusion.79
  947.9 14.8 fusion.142
  962.7 18.1 convolution_add_fusion.1
  995.4 22.1 convolution_add_fusion
  1052.5 39.9 %all-reduce.18 = (f32[1280]{0:T(1024)S(1)}, f32[1280]{0:T(1024)S(1)}, f32[1280]{0:T(1024)S(1)}, f32[1280]{0:T(1024)S(1)}, f32[1280]{0:T(1024)S(1)}, /*index=5*/f...) all-reduce(f32[1280]{0:T(1024)S(1)} %add.303, ...), channel_id=14, replica_groups=mesh['dp'=8,'seq'=4] {'dp','seq'}, use_global_device_ids=true, to_apply=%region_28.29.clone | all-reduce | flops 15360 | bytes 122880
  1102.6 144.1 %reduce-scatter.5.cloned.1.call-done = f32[40,3840]{1,0:T(8,128)} async-done(((f32[1280,3840]{1,0:T(8,128)}), f32[40,3840]{1,0:T(8,128)}) %reduce-scatter.5.cloned.1.call-update) | async-done | bytes 614416 | tf_op jit(solution)/shard_map/reduce_scatter | solution.py:343
  1246.7 561.7 %reduce-scatter.9.cloned.1.call-done = f32[40,5120]{1,0:T(8,128)} async-done(((f32[1280,5120]{1,0:T(8,128)}), f32[40,5120]{1,0:T(8,128)}) %reduce-scatter.9.cloned.1.call-update) | async-done | bytes 819216 | tf_op jit(solution)/shard_map/reduce_scatter | solution.py:345
  1808.4 561.6 %reduce-scatter.11.cloned.1.call-done = f32[160,1280]{1,0:T(8,128)} async-done(((f32[5120,1280]{1,0:T(8,128)}), f32[160,1280]{1,0:T(8,128)}) %reduce-scatter.11.cloned.1.call-update) | async-done | bytes 819216 | tf_op jit(solution)/shard_map/reduce_scatter | solution.py:346
  (417 shorter events, 442.8 us)
Async XLA Ops:
  7.2 89.6 %all-gather.21.cloned.1.call-start = ((), (), s32[]{:S(2)}) async-start(), calls=%async_computation.4 | async-start | bytes 10137600 | tf_op jit(solution)/shard_map/all_gather | solution.py:276
  7.9 152.0 %all-gather.25.cloned.1.call-start = ((), (), s32[]{:S(2)}) async-start(), calls=%async_computation.6 | async-start | bytes 3276800 | tf_op jit(solution)/shard_map/all_gather | solution.py:87
  106.5 109.9 %all-gather.35.cloned.1.call-start = ((), (), s32[]{:S(2)}) async-start(), calls=%async_computation.11 | async-start | bytes 3276800 | tf_op jit(solution)/shard_map/all_gather | solution.py:87
  116.1 157.2 %all-gather.23.cloned.1.call-start = ((), (), s32[]{:S(2)}) async-start(), calls=%async_computation.5 | async-start | bytes 3276800 | tf_op jit(solution)/shard_map/all_gather | solution.py:88
  120.4 208.5 %all-gather.33.cloned.1.call-start = ((), (), s32[]{:S(2)}) async-start(), calls=%async_computation.10 | async-start | bytes 3276800 | tf_op jit(solution)/shard_map/all_gather | solution.py:88
  121.0 262.9 %all-gather.37.cloned.1.call-start = ((), (), s32[]{:S(2)}) async-start(), calls=%async_computation.12 | async-start | bytes 3276800 | tf_op jit(solution)/shard_map/all_gather | solution.py:192
  121.5 318.0 %all-gather.39.cloned.1.call-start = ((), (), s32[]{:S(2)}) async-start(), calls=%async_computation.13 | async-start | bytes 3276800 | tf_op jit(solution)/shard_map/all_gather | solution.py:192
  122.3 378.5 %all-gather.27.cloned.1.call-start = ((), (), s32[]{:S(2)}) async-start(), calls=%async_computation.7 | async-start | bytes 3379200 | tf_op jit(solution)/shard_map/all_gather | solution.py:277
  123.0 477.0 %all-gather.29.cloned.1.call-start = ((), (), s32[]{:S(2)}) async-start(), calls=%async_computation.8 | async-start | bytes 13516800 | tf_op jit(solution)/shard_map/all_gather | solution.py:278
  123.8 575.2 %all-gather.31.cloned.1.call-start = ((), (), s32[]{:S(2)}) async-start(), calls=%async_computation.9 | async-start | bytes 13516800 | tf_op jit(solution)/shard_map/all_gather | solution.py:279
  124.4 746.1 %all-gather.41.cloned.1.call-start = ((), (), s32[]{:S(2)}) async-start(), calls=%async_computation.18 | async-start | bytes 3276800 | tf_op jit(solution)/shard_map/all_gather | solution.py:193
  125.8 318.2 %copy-start.106 = (pred[1024]{0:T(1024)(128)(4,1)}, pred[1024]{0:T(1024)(128)(4,1)S(1)}, u32[]{:S(2)}) copy-start(pred[1024]{0:T(1024)(128)(4,1)S(1)} %iota_compare_fusion.1) | copy-start | bytes 3076
  126.5 378.9 %copy-start.104 = (pred[1024]{0:T(1024)(128)(4,1)}, pred[1024]{0:T(1024)(128)(4,1)S(1)}, u32[]{:S(2)}) copy-start(pred[1024]{0:T(1024)(128)(4,1)S(1)} %iota_compare_fusion) | copy-start | bytes 3076
  169.1 274.9 %copy-start.59 = (f32[20,256]{1,0:T(8,128)}, f32[20,256]{1,0:T(8,128)S(1)}, u32[]{:S(2)}) copy-start(f32[20,256]{1,0:T(8,128)S(1)} %get-tuple-element.86) | copy-start | bytes 61444
  176.1 267.9 %copy-start.63 = (f32[20,256]{1,0:T(8,128)}, f32[20,256]{1,0:T(8,128)S(1)}, u32[]{:S(2)}) copy-start(f32[20,256]{1,0:T(8,128)S(1)} %fusion.3) | copy-start | bytes 61444
  225.6 279.8 %copy-start.57 = (f32[20,256]{1,0:T(8,128)}, f32[20,256]{1,0:T(8,128)S(1)}, u32[]{:S(2)}) copy-start(f32[20,256]{1,0:T(8,128)S(1)} %get-tuple-element.81) | copy-start | bytes 61444
  232.7 272.8 %copy-start.61 = (f32[20,256]{1,0:T(8,128)}, f32[20,256]{1,0:T(8,128)S(1)}, u32[]{:S(2)}) copy-start(f32[20,256]{1,0:T(8,128)S(1)} %fusion.5) | copy-start | bytes 61444
  504.0 246.1 %copy-start.73 = (f32[256]{0:T(256)}, f32[256]{0:T(256)S(1)}, u32[]{:S(2)}) copy-start(f32[256]{0:T(256)S(1)} %broadcast_multiply_fusion.2) | copy-start | bytes 3076
  516.8 233.3 %copy-start.5 = (f32[1,256,1280]{2,1,0:T(8,128)}, f32[1,256,1280]{2,1,0:T(8,128)S(1)}, u32[]{:S(2)}) copy-start(f32[1,256,1280]{2,1,0:T(8,128)S(1)} %get-tuple-element.84) | copy-start | bytes 3932164
  756.1 117.4 %all-gather.43.cloned.1.call-start = ((), (), s32[]{:S(2)}) async-start(), calls=%async_computation.19 | async-start | bytes 3276800 | tf_op jit(solution)/shard_map/all_gather | solution.py:193
  781.6 321.0 %reduce-scatter.7.cloned.1.call-start = ((), (), s32[]{:S(2)}) async-start(), calls=%async_computation.15 | async-start | bytes 6758400 | tf_op jit(solution)/shard_map/reduce_scatter | solution.py:344
  806.1 440.6 %reduce-scatter.5.cloned.1.call-start = ((), (), s32[]{:S(2)}) async-start(), calls=%async_computation.14 | async-start | bytes 20275200 | tf_op jit(solution)/shard_map/reduce_scatter | solution.py:343
  947.3 861.1 %reduce-scatter.9.cloned.1.call-start = ((), (), s32[]{:S(2)}) async-start(), calls=%async_computation.16 | async-start | bytes 27033600 | tf_op jit(solution)/shard_map/reduce_scatter | solution.py:345
  980.8 1389.2 %reduce-scatter.11.cloned.1.call-start = ((), (), s32[]{:S(2)}) async-start(), calls=%async_computation.17 | async-start | bytes 27033600 | tf_op jit(solution)/shard_map/reduce_scatter | solution.py:346
  (108 other events, 2255.8 us)
Sparse Core Ops, SparseCore 0:
  10.8 85.9 all-gather.20
  106.6 53.2 all-gather.24
  161.5 54.8 all-gather.34
  218.4 54.8 all-gather.22
  275.3 53.5 all-gather.32
  330.3 53.5 all-gather.36
  386.0 53.5 all-gather.38
  442.3 58.3 all-gather.26
  503.6 96.3 all-gather.28
  602.7 96.2 all-gather.30
  756.2 53.2 all-gather.40
  811.5 54.8 all-gather.42
  869.3 160.1 reduce-scatter.6
  1036.4 210.2 reduce-scatter.4
  1249.4 558.9 reduce-scatter.8
  1811.2 558.7 reduce-scatter.10
where the time goes:
time: 2390 us; the launch traced here: 2380 us
  waiting for transfers between devices  1670 us (70%)
  matrix products  407 us (17%)
  blocking collectives  168 us (7%)
  local copies, waits for them, and re-layouts  74.6 us (3%)
  other arithmetic  39.4 us (2%)
    reduce_scatter x1, waiting for transfers between devices, body(): lax.psum_scatter(total_up, ('dp', 'seq'), scatter_dimension=0, tiled=True)  562 us
    reduce_scatter x1, waiting for transfers between devices, body(): lax.psum_scatter(total_down, ('dp', 'seq'), scatter_dimension=0, tiled=True)  562 us
    reduce_scatter x1, waiting for transfers between devices, body(): lax.psum_scatter(total_qkv, ('dp', 'seq'), scatter_dimension=0, tiled=True)  144 us
    dot_general x8, matrix products, contract_rows(): lax.dot_general(left, right, (((0,), (0,)), ((), ())), preferred_element_...  105 us
    all_gather x2, waiting for transfers between devices, backward_micro(): lax.all_gather(queries, 'seq', axis=1, tiled=True)  102 us
    unnamed x2, blocking collectives  83.7 us
    all_gather x2, waiting for transfers between devices, forward_micro(): lax.all_gather(value_local, 'seq', axis=1, tiled=True)  63.7 us
    dot_general x8, matrix products, times_transpose(): lax.dot_general(left, right, (((1,), (1,)), ((), ())), preferred_element_...  63.1 us
  transfers between devices with their start and end apart: 16, of which 13 were waited for; matrix products, arithmetic and copies ran while one was open for 19% of the time, Pallas kernels for 0%

commit v1 on v0

v1 whole, which is shorter than its diff:
```python
import jax
import jax.numpy as jnp
from jax import lax
from jax.experimental import pallas as pl
from jax.experimental.pallas import tpu as pltpu
from jax.sharding import Mesh
from jax.sharding import PartitionSpec as P

HEADS = 20
EPSILON = 1e-05
NEG = -1000000000.0
QB = 256
BF = jnp.bfloat16
F32 = jnp.float32
ALL = ("ya", "xb", "core", "seq")
DP = ("ya", "xb", "core")


def dot(left, right, dims, out=F32):
    return lax.dot_general(left, right, (dims, ((), ())), preferred_element_type=out)


NN = ((1,), (0,))
NT = ((1,), (1,))
TN = ((0,), (0,))


def size(name):
    return lax.axis_size(name)


def swap(values):
    return lax.ppermute(values, "core", [(0, 1), (1, 0)])


def by_core(own, other, axis):
    low = jnp.concatenate([own, other], axis=axis)
    high = jnp.concatenate([other, own], axis=axis)
    return jnp.where(lax.axis_index("core") == 0, low, high)


def pick(values, axis, which):
    return lax.dynamic_index_in_dim(values, which, axis, keepdims=False)


def normalise(values):
    mean = jnp.mean(values, axis=-1, keepdims=True)
    centered = values - mean
    inverse = lax.rsqrt(jnp.mean(centered * centered, axis=-1, keepdims=True) + EPSILON)
    return centered * inverse, inverse


def norm_back(normal, inverse, incoming, gain):
    scaled = incoming * gain
    first = jnp.mean(scaled, axis=-1, keepdims=True)
    second = jnp.mean(scaled * normal, axis=-1, keepdims=True)
    return (scaled - first - normal * second) * inverse


def route(cells, chips, step):
    pairs = []
    for core in range(2):
        for place in range(chips):
            block = (place + step) % chips
            target = (block // cells) * chips + core * cells + block % cells
            pairs.append((core * chips + place, target))
    return pairs


def to_cells(values):
    cells, rows, width = values.shape
    chips = size("seq")
    core, place = lax.axis_index("core"), lax.axis_index("seq")
    blocks = values.reshape(cells, 2, rows // 2, width).transpose(1, 0, 2, 3)
    blocks = blocks.reshape(chips, rows // 2, width)
    mine = core * cells + place % cells
    parts = []
    for step in range(chips):
        piece = pick(blocks, 0, (place + step) % chips)
        parts.append(lax.ppermute(piece, ("core", "seq"), route(cells, chips, step)))
    result = jnp.zeros((chips, rows // 2, width), values.dtype)
    for step in range(chips):
        slot = (mine - step + chips) % chips
        result = lax.dynamic_update_slice_in_dim(result, parts[step][None], slot, 0)
    return result.reshape(chips * rows // 2, width)


def from_cells(values, cells):
    chips = size("seq")
    core, place = lax.axis_index("core"), lax.axis_index("seq")
    rows = 2 * values.shape[0] // chips
    width = values.shape[1]
    blocks = values.reshape(chips, rows // 2, width)
    mine = core * cells + place % cells
    result = jnp.zeros((chips, rows // 2, width), values.dtype)
    parts = []
    for step in range(chips):
        piece = pick(blocks, 0, (mine - step + chips) % chips)
        back = [(b, a) for a, b in route(cells, chips, step)]
        parts.append(lax.ppermute(piece, ("core", "seq"), back))
    for step in range(chips):
        slot = (place + step) % chips
        result = lax.dynamic_update_slice_in_dim(result, parts[step][None], slot, 0)
    result = result.reshape(2, cells, rows // 2, width).transpose(1, 0, 2, 3)
    return result.reshape(cells, rows, width)


def reduce_axis(values, axis, name):
    count = size(name)
    if count > 4:
        return lax.psum_scatter(values, name, scatter_dimension=axis, tiled=False)
    index = lax.axis_index(name)
    parts = []
    for step in range(1, count):
        piece = pick(values, axis, (index + step) % count)
        pairs = [(j, (j + step) % count) for j in range(count)]
        parts.append(lax.ppermute(piece, name, pairs))
    total = pick(values, axis, index).astype(F32)
    for part in parts:
        total = total + part.astype(F32)
    return total.astype(values.dtype)


def reduce_chips(values, seq_axis):
    half = values.shape[-1] // 2
    first = reduce_axis(reduce_axis(values[..., :half], 0, "ya"), 0, "xb")
    second = reduce_axis(reduce_axis(values[..., half:], 1, "xb"), 0, "ya")
    first = reduce_axis(first, seq_axis, "seq")
    second = reduce_axis(second, seq_axis, "seq")
    return jnp.concatenate([first, second], axis=-1)


def reduce_columns(grad, parts):
    ya, xb, chips = size("ya"), size("xb"), size("seq")
    rows = grad.shape[0] // (ya * xb * 2 * chips)
    core = lax.axis_index("core")
    done = reduce_chips(grad.reshape(ya, xb, 2, chips, rows, -1), 1)
    own = pick(done, 0, core).reshape(rows, parts, 1, -1)
    other = swap(pick(done, 0, 1 - core)).reshape(rows, parts, 1, -1)
    return by_core(own, other, 2).reshape(rows, -1).astype(F32)


def forward_kernel(q_ref, k_ref, v_ref, mask_ref, o_ref, lse_ref):
    rows, lanes = q_ref.shape
    dim = lanes // 2
    scale = dim ** (-0.5)
    valid = mask_ref[...] > 0
    for head in range(2):
        part = slice(head * dim, (head + 1) * dim)
        keys = k_ref[:, part]
        turned = v_ref[:, part].T

        def block(index, carry):
            start = pl.multiple_of(index * QB, QB)
            queries = q_ref[pl.ds(start, QB), part] * BF(scale)
            scores = jnp.where(valid, dot(keys, queries, NT), NEG)
            top = jnp.max(scores, axis=0, keepdims=True)
            exponent = jnp.exp(scores - top)
            total = jnp.sum(exponent, axis=0, keepdims=True)
            mixed = dot(turned, exponent.astype(BF), NN) / total
            o_ref[pl.ds(start, QB), part] = mixed.T.astype(BF)
            lse_ref[0, head : head + 1, pl.ds(start, QB)] = top + jnp.log(total)
            return carry

        lax.fori_loop(0, rows // QB, block, 0)


def backward_kernel(q_ref, k_ref, v_ref, d_ref, lse_ref, mask_ref, out_ref, dk_ref, dv_ref):
    rows, lanes = q_ref.shape
    dim = lanes // 2
    scale = dim ** (-0.5)
    valid = mask_ref[...] > 0
    for head in range(2):
        part = slice(head * dim, (head + 1) * dim)
        keys = k_ref[:, part]
        values = v_ref[:, part]
        turned = keys.T
        dk_ref[...] = jnp.zeros_like(dk_ref)
        dv_ref[...] = jnp.zeros_like(dv_ref)

        def block(index, carry):
            start = pl.multiple_of(index * QB, QB)
            queries = q_ref[pl.ds(start, QB), part] * BF(scale)
            incoming = d_ref[pl.ds(start, QB), part]
            lse = lse_ref[0, head : head + 1, pl.ds(start, QB)]
            scores = jnp.where(valid, dot(keys, queries, NT), NEG)
            soft = jnp.exp(scores - lse)
            d_soft = dot(values, incoming, NT)
            inner = jnp.sum(soft * d_soft, axis=0, keepdims=True)
            d_scores = (soft * (d_soft - inner)).astype(BF)
            dv_ref[...] += dot(soft.astype(BF), incoming, NN)
            dk_ref[...] += dot(d_scores, queries, NN)
            d_queries = dot(turned, d_scores, NN) * scale
            out_ref[0, pl.ds(start, QB), part] = d_queries.T.astype(BF)
            return carry

        lax.fori_loop(0, rows // QB, block, 0)
        out_ref[1, :, part] = dk_ref[...].astype(BF)
        out_ref[2, :, part] = dv_ref[...].astype(BF)


def attend(project, mask):
    rows, columns = project.shape
    width = columns // 3
    pair = 2 * 64
    pairs = width // pair
    cost = pl.CostEstimate(
        flops=4 * rows * rows * width, bytes_accessed=8 * rows * width, transcendentals=0
    )
    return pl.pallas_call(
        forward_kernel,
        grid=(pairs,),
        in_specs=[
            pl.BlockSpec((rows, pair), lambda j: (0, j)),
            pl.BlockSpec((rows, pair), lambda j: (0, pairs + j)),
            pl.BlockSpec((rows, pair), lambda j: (0, 2 * pairs + j)),
            pl.BlockSpec((rows, QB), lambda j: (0, 0)),
        ],
        out_specs=[
            pl.BlockSpec((rows, pair), lambda j: (0, j)),
            pl.BlockSpec((1, 2, rows), lambda j: (j, 0, 0)),
        ],
        out_shape=[
            jax.ShapeDtypeStruct((rows, width), BF),
            jax.ShapeDtypeStruct((pairs, 2, rows), F32),
        ],
        cost_estimate=cost,
        name="attend",
    )(project, project, project, mask)


def attend_back(project, incoming, lse, mask):
    rows, columns = project.shape
    width = columns // 3
    pair = 2 * 64
    pairs = width // pair
    cost = pl.CostEstimate(
        flops=10 * rows * rows * width, bytes_accessed=14 * rows * width, transcendentals=0
    )
    return pl.pallas_call(
        backward_kernel,
        grid=(pairs,),
        in_specs=[
            pl.BlockSpec((rows, pair), lambda j: (0, j)),
            pl.BlockSpec((rows, pair), lambda j: (0, pairs + j)),
            pl.BlockSpec((rows, pair), lambda j: (0, 2 * pairs + j)),
            pl.BlockSpec((rows, pair), lambda j: (0, j)),
            pl.BlockSpec((1, 2, rows), lambda j: (j, 0, 0)),
            pl.BlockSpec((rows, QB), lambda j: (0, 0)),
        ],
        out_specs=pl.BlockSpec((3, rows, pair), lambda j: (0, 0, j)),
        out_shape=jax.ShapeDtypeStruct((3, rows, width), BF),
        scratch_shapes=[pltpu.VMEM((rows, pair // 2), F32), pltpu.VMEM((rows, pair // 2), F32)],
        cost_estimate=cost,
        name="attend_back",
    )(project, project, project, incoming, lse, mask)


def body(tokens, lengths, cotangent, w_qkv, w_out, w_up, w_down, *small):
    cells, rows_local, width = tokens.shape
    ya, xb, chips = size("ya"), size("xb"), size("seq")
    core, place = lax.axis_index("core"), lax.axis_index("seq")
    chip_pairs = ya * xb
    half = width // 2
    own_rows = chips * rows_local // 2
    sizes = [member.shape[0] for member in small]

    packed = lax.all_gather(jnp.concatenate(small)[None], ALL, axis=0, tiled=True)
    vectors, at = [], 0
    for count in sizes:
        vectors.append(packed[:, at : at + count].reshape(-1).astype(F32))
        at += count
    (
        gain_one, shift_one, bias_query, bias_value, bias_out,
        gain_two, shift_two, bias_up, bias_down,
    ) = vectors
    full_qkv = lax.all_gather(w_qkv, ALL, axis=0, tiled=True)
    qkv = pick(full_qkv.reshape(width, 3, 2, half), 2, core).reshape(width, 3 * half)
    out_full = lax.all_gather(w_out, ALL, axis=0, tiled=True)
    full_up = lax.all_gather(w_up, ALL, axis=0, tiled=True)
    hidden_all = full_up.shape[1]
    up = pick(full_up.reshape(width, chip_pairs, 2, -1), 2, core).reshape(width, hidden_all // 2)
    down = lax.all_gather(w_down, ("ya", "xb", "seq"), axis=0, tiled=True)
    up_bias = pick(bias_up.reshape(chip_pairs, 2, -1), 1, core).reshape(-1)
    project_bias = jnp.concatenate(
        [
            pick(bias_query.reshape(2, half), 0, core),
            jnp.zeros((half,), F32),
            pick(bias_value.reshape(2, half), 0, core),
        ]
    )

    inputs = to_cells(tokens)
    incoming = to_cells(cotangent)
    other_counts = swap(lengths)
    counts = jnp.where(core == 0, jnp.concatenate([lengths, other_counts]), jnp.concatenate([other_counts, lengths]))
    count = lax.dynamic_index_in_dim(counts, place, 0, keepdims=False)
    row = jnp.arange(2 * own_rows)
    holder = jnp.where(row < own_rows, core, 1 - core)
    row = row % own_rows
    position = (row // (rows_local // 2)) * rows_local + holder * (rows_local // 2) + row % (rows_local // 2)
    mask = jnp.broadcast_to((position < count).astype(F32)[:, None], (2 * own_rows, QB))

    inputs = inputs.astype(F32)
    normal_one, inverse_one = normalise(inputs)
    normed_low = (normal_one * gain_one + shift_one).astype(BF)
    normed_all = jnp.concatenate([normed_low, swap(normed_low)], axis=0)
    project = (dot(normed_all, qkv, NN) + project_bias).astype(BF)
    mixed_heads, lse = attend(project, mask)
    mixed_own = by_core(mixed_heads[:own_rows], swap(mixed_heads[own_rows:]), 1)
    middle = inputs + (dot(mixed_own, out_full, NN) + bias_out)
    normal_two, inverse_two = normalise(middle)
    second_low = (normal_two * gain_two + shift_two).astype(BF)
    second_all = jnp.concatenate([second_low, swap(second_low)], axis=0)
    hidden = dot(second_all, up, NN) + up_bias
    half_erf = 0.5 * (1.0 + lax.erf(hidden * (0.5**0.5)))
    active = (hidden * half_erf).astype(BF)
    slope = (half_erf + hidden * jnp.exp(-0.5 * hidden * hidden) * 0.3989422804014327).astype(BF)
    branch_own = dot(active[:own_rows], down, NN)
    branch_other = swap(dot(active[own_rows:], down, NN).astype(BF))
    output = (middle + (branch_own + branch_other.astype(F32) + bias_down)).astype(BF)
    output = from_cells(output, cells)

    incoming_all = jnp.concatenate([incoming, swap(incoming)], axis=0)
    grad_bias_down = jnp.sum(incoming.astype(F32), axis=0)
    d_hidden = (dot(incoming_all, down, NT) * slope.astype(F32)).astype(BF)
    grad_down = dot(active, incoming_all, TN, BF)
    grad_down = reduce_chips(grad_down.reshape(ya, xb, chips, -1, width), 0).astype(F32)
    grad_up = reduce_columns(dot(second_all, d_hidden, TN, BF), chip_pairs)
    grad_bias_up = jnp.sum(d_hidden.astype(F32), axis=0)
    d_second = dot(d_hidden[:own_rows], up, NT) + swap(
        dot(d_hidden[own_rows:], up, NT).astype(BF)
    ).astype(F32)
    d_middle = incoming.astype(F32) + norm_back(normal_two, inverse_two, d_second, gain_two)
    grad_gain_two = jnp.sum(d_second * normal_two, axis=0)
    grad_shift_two = jnp.sum(d_second, axis=0)
    d_attend = d_middle.astype(BF)
    grad_bias_out = jnp.sum(d_attend.astype(F32), axis=0)
    d_mixed = dot(d_attend, out_full, NT).astype(BF)
    low, high = d_mixed[:, :half], d_mixed[:, half:]
    d_mixed_heads = jnp.concatenate(
        [jnp.where(core == 0, low, high), swap(jnp.where(core == 0, high, low))], axis=0
    )
    d_project = attend_back(project, d_mixed_heads, lse, mask)

    low, high = d_attend[:, :half], d_attend[:, half:]
    d_attend_columns = jnp.concatenate(
        [jnp.where(core == 0, low, high), swap(jnp.where(core == 0, high, low))], axis=0
    )
    mixed_other = by_core(mixed_heads[own_rows:], swap(mixed_heads[:own_rows]), 1)
    mixed_all = jnp.concatenate([mixed_own, mixed_other], axis=0)
    grad_out = reduce_columns(dot(mixed_all, d_attend_columns, TN, BF), 1)

    sides = jnp.sum(d_project.astype(F32), axis=1)
    flat = jnp.concatenate([d_project[0], d_project[1], d_project[2]], axis=1)
    d_normed = dot(flat[:own_rows], qkv, NT) + swap(dot(flat[own_rows:], qkv, NT).astype(BF)).astype(F32)
    grad_qkv = reduce_columns(dot(normed_all, flat, TN, BF), 3)
    input_grad = d_middle + norm_back(normal_one, inverse_one, d_normed, gain_one)
    input_grad = from_cells(input_grad.astype(BF), cells).astype(F32)
    grad_gain_one = jnp.sum(d_normed * normal_one, axis=0)
    grad_shift_one = jnp.sum(d_normed, axis=0)

    own_half = (jnp.arange(2) == core).astype(F32)
    totals = (
        grad_gain_one,
        grad_shift_one,
        own_half[:, None] * sides[0],
        own_half[:, None] * sides[2],
        grad_bias_out,
        grad_gain_two,
        grad_shift_two,
        own_half[:, None] * grad_bias_up.reshape(chip_pairs, 1, -1),
        grad_bias_down,
    )
    packed = jnp.concatenate([total.reshape(ya, xb, 2, chips, -1) for total in totals], axis=-1)
    packed = reduce_axis(packed, 2, "core")
    packed = reduce_axis(packed, 0, "ya")
    packed = reduce_axis(packed, 0, "xb")
    packed = reduce_axis(packed, 0, "seq")
    smalls, at = [], 0
    for count in sizes:
        smalls.append(packed[at : at + count])
        at += count
    return (output, input_grad, grad_qkv, grad_out, grad_up, grad_down, *smalls)


def solution(mesh):
    pairs, chips = mesh.devices.shape[0] // 2, mesh.devices.shape[1]
    fine = Mesh(mesh.devices.reshape(pairs // 2, 2, 2, chips), ALL)
    rows = P(DP, "seq", None)
    matrix = P(ALL, None)
    vector = P(ALL)
    return jax.shard_map(
        body,
        mesh=fine,
        in_specs=(rows, P(DP), rows) + (matrix,) * 4 + (vector,) * 9,
        out_specs=(rows, rows) + (matrix,) * 4 + (vector,) * 9,
        check_vma=False,
    )
```

time: 2390 us -> 853 us (0.36)
  waiting for transfers between devices: 1670 us -> 278 us
  matrix products: 407 us -> 112 us
  starting transfers between devices: 0.98 us -> 133 us
  blocking collectives: 168 us -> 68.9 us
  Pallas kernels: 0 us -> 92.5 us
  local copies, waits for them, and re-layouts: 74.6 us -> 104 us
    reduce_scatter x4 -> x0, waiting for transfers between devices: 1270 us -> none  [the longest x1 562 us: body(): lax.psum_scatter(total_up, ('dp', 'seq'), scatter_dimension=0, tiled=True)]
    dot_general x38 -> x15, matrix products: 407 us -> 112 us  [dot(): lax.dot_general(left, right, (dims, ((), ())), preferred_element_type=out)]
    all_gather x12 -> x4, waiting for transfers between devices: 400 us -> 141 us  [the longest x1 73.4 us: body(): full_up = lax.all_gather(w_up, ALL, axis=0, tiled=True)]
    ppermute x0 -> x76, waiting for transfers between devices: none -> 135 us  [the longest x46 130 us: reduce_axis(): parts.append(lax.ppermute(piece, name, pairs))]
    ppermute x0 -> x76, starting transfers between devices: none -> 133 us  [the longest x46 90.8 us: reduce_axis(): parts.append(lax.ppermute(piece, name, pairs))]
    pallas_call x0 -> x2, Pallas kernels: none -> 92.5 us  [the longest x1 50.2 us: attend_back(): pl.pallas_call(backward_kernel, grid=(pairs,), in_specs=[pl.BlockSpec((ro...]
    all_gather x6 -> x0, blocking collectives: 83.9 us -> none  [the longest x2 28 us: backward_micro(): lax.all_gather(saved_residual['row_max'][..., 0].astype(jnp.bfloat16), 's...]
    unnamed x2 -> x1, blocking collectives: 83.7 us -> 68.9 us
  transfers between devices with their start and end apart: 16 -> 80, of which waited for: 13 -> 26; matrix products, arithmetic and copies ran while one was open for 19% -> 27% of each run, Pallas kernels for 0% -> 11%
where the time goes in v1:
time: 853 us; the launch traced here: 847 us
  waiting for transfers between devices  278 us (33%)
  starting transfers between devices  133 us (16%)
  matrix products  112 us (13%)
  local copies, waits for them, and re-layouts  104 us (12%)
  Pallas kernels  92.5 us (11%)
  blocking collectives  68.9 us (8%)
  other arithmetic  43.6 us (5%)
  between operations  15.8 us (2%)
    ppermute x46, waiting for transfers between devices, reduce_axis(): parts.append(lax.ppermute(piece, name, pairs))  130 us
    dot_general x15, matrix products, dot(): lax.dot_general(left, right, (dims, ((), ())), preferred_element_type=out)  112 us
    ppermute x46, starting transfers between devices, reduce_axis(): parts.append(lax.ppermute(piece, name, pairs))  90.8 us
    all_gather x1, waiting for transfers between devices, body(): full_up = lax.all_gather(w_up, ALL, axis=0, tiled=True)  73.4 us
    unnamed x1, blocking collectives  68.9 us
    all_gather x1, waiting for transfers between devices, body(): down = lax.all_gather(w_down, ('ya', 'xb', 'seq'), axis=0, tiled=True)  65.3 us
    pallas_call x1, Pallas kernels, attend_back(): pl.pallas_call(backward_kernel, grid=(pairs,), in_specs=[pl.BlockSpec((ro...  50.2 us
    pallas_call x1, Pallas kernels, attend(): pl.pallas_call(forward_kernel, grid=(pairs,), in_specs=[pl.BlockSpec((row...  42.3 us
  transfers between devices with their start and end apart: 80, of which 26 were waited for; matrix products, arithmetic and copies ran while one was open for 27% of the time, Pallas kernels for 11%

profile of v1, /device:TPU:0, one launch (start us, length us, event | category | flops | bytes accessed | tf_op | source)
XLA Modules:
  0.0 846.7 jit_solution(17382079348187442536)
XLA Ops:
  21.3 68.9 %all-reduce = bf16[15360]{0:T(1024)(128)(2,1)S(1)} all-reduce(bf16[15360]{0:T(1024)(128)(2,1)S(1)} %dynamic-update-slice), channel_id=2, replica_groups=mesh['ya'=2,'xb'=2,'core'=2,'seq'=4] {'ya','xb','core','seq'}, use_global_device_ids=true, to_apply=%add | all-reduce | flops 15360 | bytes 61440
  109.5 13.7 %copy.79 = bf16[1280,3840]{0,1:T(8,128)(2,1)} copy(bf16[1280,3840]{1,0:T(8,128)(2,1)} %all-gather.6.cloned.1.call-done) | data formatting | bytes 19660800 | tf_op jit(solution)/shard_map/all_gather | solution.py:277
  125.9 10.6 %add_convert_fusion.q_ref.k_ref.v_ref = bf16[1024,1920]{1,0:T(8,128)(2,1)} fusion(f32[1920]{0:T(1024)S(1)} %pad_maximum_fusion.11, bf16[1280,1920]{0,1:T(8,128)(2,1)S(1)} %bitcast.358, bf16[512,1280]{1,0:T(8,128)(2,1)} %collective-permute-done.4, bf16[512,1280]{1,0:T(8,128)(2,1)} %add_convert_fusion.4), kind=kOutput, calls=%fused_computation.11 | convolution fusion | flops 5042339840 | bytes 11476480 | tf_op jit(solution)/shard_map/dot_general | solution.py:20
  137.7 42.3 %attend.1 = (bf16[1024,640]{1,0:T(8,128)(2,1)}, f32[5,2,1024]{2,1,0:T(2,128)}) custom-call(bf16[1024,1920]{1,0:T(8,128)(2,1)} %add_convert_fusion.q_ref.k_ref.v_ref, bf16[1024,1920]{1,0:T(8,128)(2,1)} %add_convert_fusion.q_ref.k_ref.v_ref, bf16[1024,1920]{1,0:T(8,128)(2,1)} %add_convert_fusion.q_ref.k_ref.v_ref, f32[1024,256]{1,0:T(8,128)} %broadcast_in_dim.95.mask_ref), custom_call_target="tpu_custom_call" | custom-call | flops 2684354560 | bytes 5242880 | tf_op jit(solution)/shard_map/attend/pallas_call | solution.py:210
  200.0 73.4 %all-gather.10.cloned.1.call-done = bf16[1280,5120]{1,0:T(8,128)(2,1)} async-done(((bf16[40,5120]{1,0:T(8,128)(2,1)}), bf16[1280,5120]{1,0:T(8,128)(2,1)}) %all-gather.10.cloned.1.call-update) | async-done | bytes 13107216 | tf_op jit(solution)/shard_map/all_gather | solution.py:280
  273.5 17.7 %copy.80 = bf16[1280,5120]{0,1:T(8,128)(2,1)} copy(bf16[1280,5120]{1,0:T(8,128)(2,1)} %all-gather.10.cloned.1.call-done) | data formatting | bytes 26214400 | tf_op jit(solution)/shard_map/all_gather | solution.py:280
  294.4 10.7 %multiply_convert_fusion.1 = (bf16[1024,2560]{1,0:T(8,128)(2,1)}, f32[1024,2560]{1,0:T(8,128)}) fusion(f32[2560]{0:T(1024)S(1)} %add.712, bf16[1280,2560]{0,1:T(8,128)(2,1)S(1)} %bitcast.343, bf16[512,1280]{1,0:T(8,128)(2,1)} %collective-permute-done.7, bf16[512,1280]{1,0:T(8,128)(2,1)S(1)} %add_convert_fusion.3), kind=kOutput, calls=%fused_computation.8 | convolution fusion | flops 6731857920 | bytes 24913920 | tf_op jit(solution)/shard_map/dot_general | solution.py:20
  305.2 65.3 %all-gather.12.cloned.1.call-done = bf16[2560,1280]{1,0:T(8,128)(2,1)} async-done(((bf16[160,1280]{1,0:T(8,128)(2,1)}), bf16[2560,1280]{1,0:T(8,128)(2,1)}) %all-gather.12.cloned.1.call-update) | async-done | bytes 6553616 | tf_op jit(solution)/shard_map/all_gather | solution.py:283
  370.5 15.0 %convert_reduce_fusion = (f32[2560]{0:T(1024)S(1)}, bf16[1024,2560]{1,0:T(8,128)(2,1)}) fusion(f32[1024,2560]{1,0:T(8,128)} %get-tuple-element.136, f32[2560]{0:T(1024)S(1)} %add.712, bf16[2560,1280]{1,0:T(8,128)(2,1)} %all-gather.12.cloned.1.call-done, bf16[512,1280]{1,0:T(8,128)(2,1)} %collective-permute-done.17, bf16[512,1280]{1,0:T(8,128)(2,1)S(1)} %bitcast.354), kind=kOutput, calls=%fused_computation.6 | convolution fusion | flops 6755448320 | bytes 24924160 | tf_op jit(solution)/shard_map/dot_general | solution.py:20
  397.3 9.4 %fusion.28 = bf16[2560,1280]{1,0:T(8,128)(2,1)S(1)} fusion(bf16[1024,2560]{1,0:T(8,128)(2,1)} %get-tuple-element.135, bf16[512,1280]{1,0:T(8,128)(2,1)} %collective-permute-done.17, bf16[512,1280]{1,0:T(8,128)(2,1)S(1)} %bitcast.355), kind=kOutput, calls=%fused_computation.68 | convolution fusion | flops 6716129280 | bytes 14417920 | tf_op jit(solution)/shard_map/dot_general | solution.py:20
  412.0 10.1 %fusion.29 = bf16[1280,2560]{1,0:T(8,128)(2,1)S(1)} fusion(bf16[1024,2560]{1,0:T(8,128)(2,1)} %get-tuple-element.139, bf16[512,1280]{1,0:T(8,128)(2,1)} %collective-permute-done.7, bf16[512,1280]{1,0:T(8,128)(2,1)S(1)} %copy-done.32), kind=kOutput, calls=%fused_computation.69 | convolution fusion | flops 6716129280 | bytes 14417920 | tf_op jit(solution)/shard_map/dot_general | solution.py:20
  437.5 8.5 convert_reduce_fusion.3
  455.7 28.6 %collective-permute-done.54 = bf16[2,2,4,40,1280]{4,3,1,2,0:T(8,128)(2,1)} collective-permute-done((bf16[2,2,4,40,1280]{4,3,1,2,0:T(8,128)(2,1)}, bf16[2,2,4,40,1280]{4,3,1,2,0:T(8,128)(2,1)}, u32[]{:S(2)}, u32[]{:S(2)}) %collective-permute-start.54) | collective-permute-done | bytes 1638432 | tf_op jit(solution)/shard_map/ppermute | solution.py:117
  506.8 50.2 %attend_back.1 = bf16[3,1024,640]{2,1,0:T(8,128)(2,1)} custom-call(bf16[1024,1920]{1,0:T(8,128)(2,1)} %add_convert_fusion.q_ref.k_ref.v_ref, bf16[1024,1920]{1,0:T(8,128)(2,1)} %add_convert_fusion.q_ref.k_ref.v_ref, bf16[1024,1920]{1,0:T(8,128)(2,1)} %add_convert_fusion.q_ref.k_ref.v_ref, bf16[1024,640]{1,0:T(8,128)(2,1)} %pad_maximum_fusion.10.d_ref, ...), custom_call_target="tpu_custom_call" | custom-call | flops 6710886400 | bytes 9175040 | tf_op jit(solution)/shard_map/attend_back/pallas_call | solution.py:240
  575.3 8.3 fusion.31
  606.3 21.0 %collective-permute-done.44 = bf16[2,4,40,320]{3,2,0,1:T(8,128)(2,1)S(1)} collective-permute-done((bf16[2,4,40,320]{3,2,0,1:T(8,128)(2,1)S(1)}, bf16[2,4,40,320]{3,2,0,1:T(8,128)(2,1)S(1)}, u32[]{:S(2)}, u32[]{:S(2)}) %collective-permute-start.44) | collective-permute-done | bytes 204832 | tf_op jit(solution)/shard_map/ppermute | solution.py:117
  627.4 8.8 %collective-permute-start.45 = (bf16[2,40,320]{2,1,0:T(8,128)(2,1)S(1)}, bf16[2,40,320]{2,1,0:T(8,128)(2,1)S(1)}, u32[]{:S(2)}, u32[]{:S(2)}) collective-permute-start(bf16[2,40,320]{2,1,0:T(8,128)(2,1)S(1)} %get-tuple-element.100), channel_id=1, source_target_pairs={{0,1},{1,2},{2,3},{3,0},{4,5},{5,6},{6,7},{7,4},{8,9},{9,10},{10,1... | collective-permute-start | bytes 153608 | tf_op jit(solution)/shard_map/ppermute | solution.py:117
  665.1 8.8 %collective-permute-done.57 = bf16[2,40,1280]{2,1,0:T(8,128)(2,1)S(1)} collective-permute-done((bf16[2,40,1280]{2,1,0:T(8,128)(2,1)S(1)}, bf16[2,40,1280]{2,1,0:T(8,128)(2,1)S(1)}, u32[]{:S(2)}, u32[]{:S(2)}) %collective-permute-start.57) | collective-permute-done | bytes 204832 | tf_op jit(solution)/shard_map/ppermute | solution.py:117
  674.0 9.2 %collective-permute-start.53 = (bf16[2,40,1280]{2,1,0:T(8,128)(2,1)S(1)}, bf16[2,40,1280]{2,1,0:T(8,128)(2,1)S(1)}, u32[]{:S(2)}, u32[]{:S(2)}) collective-permute-start(bf16[2,40,1280]{2,1,0:T(8,128)(2,1)S(1)} %get-tuple-element.88), channel_id=1, source_target_pairs={{0,3},{1,0},{2,1},{3,2},{4,7},{5,4},{6,5},{7,6},{8,11},{9,8},{10,9... | collective-permute-start | bytes 614408 | tf_op jit(solution)/shard_map/ppermute | solution.py:117
  697.5 9.4 %collective-permute-start.67 = (bf16[160,640]{1,0:T(8,128)(2,1)S(1)}, bf16[160,640]{1,0:T(8,128)(2,1)S(1)}, u32[]{:S(2)}, u32[]{:S(2)}) collective-permute-start(bf16[160,640]{1,0:T(8,128)(2,1)S(1)} %get-tuple-element.81), channel_id=1, source_target_pairs={{0,1},{1,2},{2,3},{3,0},{4,5},{5,6},{6,7},{7,4},{8,9},{9,10},{10,1... | collective-permute-start | bytes 614408 | tf_op jit(solution)/shard_map/ppermute | solution.py:117
  716.6 8.7 %collective-permute-done.68 = bf16[160,640]{1,0:T(8,128)(2,1)S(1)} collective-permute-done((bf16[160,640]{1,0:T(8,128)(2,1)S(1)}, bf16[160,640]{1,0:T(8,128)(2,1)S(1)}, u32[]{:S(2)}, u32[]{:S(2)}) %collective-permute-start.68) | collective-permute-done | bytes 204832 | tf_op jit(solution)/shard_map/ppermute | solution.py:117
  773.3 11.4 %collective-permute-start.23 = (bf16[128,1280]{1,0:T(8,128)(2,1)S(1)}, bf16[128,1280]{1,0:T(8,128)(2,1)S(1)}, u32[]{:S(2)}, u32[]{:S(2)}) collective-permute-start(bf16[128,1280]{1,0:T(8,128)(2,1)S(1)} %get-tuple-element.55), channel_id=1, source_target_pairs={{4,0},{5,1},{0,2},{1,3},{6,4},{7,5},{2,6},{3,7},{12,8},{13,9},{8,1... | collective-permute-start | bytes 983048 | tf_op jit(solution)/shard_map/ppermute | solution.py:100
  805.5 10.4 %collective-permute-done.33 = bf16[2,40,960]{2,1,0:T(8,128)(2,1)S(1)} collective-permute-done((bf16[2,40,960]{2,1,0:T(8,128)(2,1)S(1)}, bf16[2,40,960]{2,1,0:T(8,128)(2,1)S(1)}, u32[]{:S(2)}, u32[]{:S(2)}) %collective-permute-start.33) | collective-permute-done | bytes 153632 | tf_op jit(solution)/shard_map/ppermute | solution.py:117
  818.4 9.9 %collective-permute-done.28 = bf16[2,40,960]{2,1,0:T(8,128)(2,1)S(1)} collective-permute-done((bf16[2,40,960]{2,1,0:T(8,128)(2,1)S(1)}, bf16[2,40,960]{2,1,0:T(8,128)(2,1)S(1)}, u32[]{:S(2)}, u32[]{:S(2)}) %collective-permute-start.28) | collective-permute-done | bytes 153632 | tf_op jit(solution)/shard_map/ppermute | solution.py:117
  (480 shorter events, 300.9 us)
Async XLA Ops:
  7.2 102.3 %all-gather.6.cloned.1.call-start = ((), (), s32[]{:S(2)}) async-start(), calls=%async_computation | async-start | bytes 10137600 | tf_op jit(solution)/shard_map/all_gather | solution.py:277
  7.9 180.8 %all-gather.8.cloned.1.call-start = ((), (), s32[]{:S(2)}) async-start(), calls=%async_computation.1 | async-start | bytes 3379200 | tf_op jit(solution)/shard_map/all_gather | solution.py:279
  8.7 264.8 %all-gather.10.cloned.1.call-start = ((), (), s32[]{:S(2)}) async-start(), calls=%async_computation.2 | async-start | bytes 13516800 | tf_op jit(solution)/shard_map/all_gather | solution.py:280
  9.4 361.1 %all-gather.12.cloned.1.call-start = ((), (), s32[]{:S(2)}) async-start(), calls=%async_computation.3 | async-start | bytes 6963200 | tf_op jit(solution)/shard_map/all_gather | solution.py:283
  12.0 80.5 %collective-permute-start = (bf16[128,1280]{1,0:T(8,128)(2,1)}, bf16[128,1280]{1,0:T(8,128)(2,1)}, u32[]{:S(2)}, u32[]{:S(2)}) collective-permute-start(bf16[128,1280]{1,0:T(8,128)(2,1)} %get-tuple-element.73), channel_id=1, source_target_pairs={{0,0},{1,1},{2,4},{3,5},{4,2},{5,3},{6,6},{7,7},{8,8},{9,9},{10,12... | collective-permute-start | bytes 983048 | tf_op jit(solution)/shard_map/ppermute | solution.py:80
  15.9 78.4 %collective-permute-start.1 = (bf16[128,1280]{1,0:T(8,128)(2,1)}, bf16[128,1280]{1,0:T(8,128)(2,1)}, u32[]{:S(2)}, u32[]{:S(2)}) collective-permute-start(bf16[128,1280]{1,0:T(8,128)(2,1)} %get-tuple-element.72), channel_id=1, source_target_pairs={{0,1},{1,4},{2,5},{3,0},{4,3},{5,6},{6,7},{7,2},{8,9},{9,12},{10,1... | collective-permute-start | bytes 983048 | tf_op jit(solution)/shard_map/ppermute | solution.py:80
  18.9 76.5 %collective-permute-start.2 = (bf16[128,1280]{1,0:T(8,128)(2,1)S(1)}, bf16[128,1280]{1,0:T(8,128)(2,1)}, u32[]{:S(2)}, u32[]{:S(2)}) collective-permute-start(bf16[128,1280]{1,0:T(8,128)(2,1)S(1)} %get-tuple-element.71), channel_id=1, source_target_pairs={{0,4},{1,5},{2,0},{3,1},{4,6},{5,7},{6,2},{7,3},{8,12},{9,13},{10,... | collective-permute-start | bytes 983048 | tf_op jit(solution)/shard_map/ppermute | solution.py:80
  19.2 80.2 %collective-permute-start.3 = (bf16[128,1280]{1,0:T(8,128)(2,1)S(1)}, bf16[128,1280]{1,0:T(8,128)(2,1)}, u32[]{:S(2)}, u32[]{:S(2)}) collective-permute-start(bf16[128,1280]{1,0:T(8,128)(2,1)S(1)} %get-tuple-element.70), channel_id=1, source_target_pairs={{0,5},{1,0},{2,1},{3,4},{4,7},{5,2},{6,3},{7,6},{8,13},{9,8},{10,9... | collective-permute-start | bytes 983048 | tf_op jit(solution)/shard_map/ppermute | solution.py:80
  20.7 82.2 %collective-permute-start.5 = (s32[2]{0:T(128)S(1)}, s32[2]{0:T(128)S(1)}, u32[]{:S(2)}, u32[]{:S(2)}) collective-permute-start(s32[2]{0:T(128)S(1)} %copy-done.49), channel_id=1, source_target_pairs={{0,4},{4,0},{1,5},{5,1},{2,6},{6,2},{3,7},{7,3},{8,12},{12,8},{9,1... | collective-permute-start | bytes 32 | tf_op jit(solution)/shard_map/ppermute | solution.py:33
  94.3 89.6 %collective-permute-start.14 = (bf16[128,1280]{1,0:T(8,128)(2,1)}, bf16[128,1280]{1,0:T(8,128)(2,1)}, u32[]{:S(2)}, u32[]{:S(2)}) collective-permute-start(bf16[128,1280]{1,0:T(8,128)(2,1)} %get-tuple-element.62), channel_id=1, source_target_pairs={{0,1},{1,4},{2,5},{3,0},{4,3},{5,6},{6,7},{7,2},{8,9},{9,12},{10,1... | collective-permute-start | bytes 983048 | tf_op jit(solution)/shard_map/ppermute | solution.py:80
  95.4 89.5 %collective-permute-start.15 = (bf16[128,1280]{1,0:T(8,128)(2,1)}, bf16[128,1280]{1,0:T(8,128)(2,1)}, u32[]{:S(2)}, u32[]{:S(2)}) collective-permute-start(bf16[128,1280]{1,0:T(8,128)(2,1)} %get-tuple-element.61), channel_id=1, source_target_pairs={{0,4},{1,5},{2,0},{3,1},{4,6},{5,7},{6,2},{7,3},{8,12},{9,13},{10,... | collective-permute-start | bytes 983048 | tf_op jit(solution)/shard_map/ppermute | solution.py:80
  102.9 92.2 %collective-permute-start.16 = (bf16[128,1280]{1,0:T(8,128)(2,1)}, bf16[128,1280]{1,0:T(8,128)(2,1)}, u32[]{:S(2)}, u32[]{:S(2)}) collective-permute-start(bf16[128,1280]{1,0:T(8,128)(2,1)} %get-tuple-element.60), channel_id=1, source_target_pairs={{0,5},{1,0},{2,1},{3,4},{4,7},{5,2},{6,3},{7,6},{8,13},{9,8},{10,9... | collective-permute-start | bytes 983048 | tf_op jit(solution)/shard_map/ppermute | solution.py:80
  194.6 99.8 %collective-permute-start.7 = (bf16[512,1280]{1,0:T(8,128)(2,1)S(1)}, bf16[512,1280]{1,0:T(8,128)(2,1)}, u32[]{:S(2)}, u32[]{:S(2)}) collective-permute-start(bf16[512,1280]{1,0:T(8,128)(2,1)S(1)} %add_convert_fusion.3), channel_id=1, source_target_pairs={{0,4},{4,0},{1,5},{5,1},{2,6},{6,2},{3,7},{7,3},{8,12},{12,8},{9,1... | collective-permute-start | bytes 3932168 | tf_op jit(solution)/shard_map/ppermute | solution.py:33
  196.1 109.1 %collective-permute-start.17 = (bf16[512,1280]{1,0:T(8,128)(2,1)S(1)}, bf16[512,1280]{1,0:T(8,128)(2,1)}, u32[]{:S(2)}, u32[]{:S(2)}) collective-permute-start(bf16[512,1280]{1,0:T(8,128)(2,1)S(1)} %bitcast.353), channel_id=1, source_target_pairs={{0,4},{4,0},{1,5},{5,1},{2,6},{6,2},{3,7},{7,3},{8,12},{12,8},{9,1... | collective-permute-start | bytes 3932168 | tf_op jit(solution)/shard_map/ppermute | solution.py:33
  411.4 80.5 %collective-permute-start.65 = (bf16[2,4,160,640]{3,2,1,0:T(8,128)(2,1)}, bf16[2,4,160,640]{3,2,1,0:T(8,128)(2,1)}, u32[]{:S(2)}, u32[]{:S(2)}) collective-permute-start(bf16[2,4,160,640]{3,2,1,0:T(8,128)(2,1)} %dynamic-slice_bitcast_fusion), channel_id=1, source_target_pairs={{0,8},{8,0},{1,9},{9,1},{2,10},{10,2},{3,11},{11,3},{4,12},{12,4},... | collective-permute-start | bytes 4915208 | tf_op jit(solution)/shard_map/ppermute | solution.py:117
  425.5 58.8 %collective-permute-start.54 = (bf16[2,2,4,40,1280]{4,3,1,2,0:T(8,128)(2,1)}, bf16[2,2,4,40,1280]{4,3,1,2,0:T(8,128)(2,1)}, u32[]{:S(2)}, u32[]{:S(2)}) collective-permute-start(bf16[2,2,4,40,1280]{4,3,1,2,0:T(8,128)(2,1)} %bitcast.334), channel_id=1, source_target_pairs={{0,8},{8,0},{1,9},{9,1},{2,10},{10,2},{3,11},{11,3},{4,12},{12,4},... | collective-permute-start | bytes 4915208 | tf_op jit(solution)/shard_map/ppermute | solution.py:117
  429.8 57.1 %collective-permute-start.49 = (bf16[2,2,4,40,1280]{4,3,1,2,0:T(8,128)(2,1)}, bf16[2,2,4,40,1280]{4,3,1,2,0:T(8,128)(2,1)}, u32[]{:S(2)}, u32[]{:S(2)}) collective-permute-start(bf16[2,2,4,40,1280]{4,3,1,2,0:T(8,128)(2,1)} %bitcast.335), channel_id=1, source_target_pairs={{0,16},{16,0},{1,17},{17,1},{2,18},{18,2},{3,19},{19,3},{4,20},{20... | collective-permute-start | bytes 4915208 | tf_op jit(solution)/shard_map/ppermute | solution.py:117
  452.8 113.9 %collective-permute-start.37 = (bf16[512,640]{1,0:T(8,128)(2,1)}, bf16[512,640]{1,0:T(8,128)(2,1)}, u32[]{:S(2)}, u32[]{:S(2)}) collective-permute-start(bf16[512,640]{1,0:T(8,128)(2,1)} %get-tuple-element.53), channel_id=1, source_target_pairs={{0,4},{4,0},{1,5},{5,1},{2,6},{6,2},{3,7},{7,3},{8,12},{12,8},{9,1... | collective-permute-start | bytes 1966088 | tf_op jit(solution)/shard_map/ppermute | solution.py:33
  496.6 99.3 %collective-permute-start.61 = (bf16[4,160,640]{2,1,0:T(8,128)(2,1)}, bf16[4,160,640]{2,1,0:T(8,128)(2,1)}, u32[]{:S(2)}, u32[]{:S(2)}) collective-permute-start(bf16[4,160,640]{2,1,0:T(8,128)(2,1)} %dynamic-slice_bitcast_fusion.3), channel_id=1, source_target_pairs={{0,8},{8,0},{1,9},{9,1},{2,10},{10,2},{3,11},{11,3},{4,12},{12,4},... | collective-permute-start | bytes 2457608 | tf_op jit(solution)/shard_map/ppermute | solution.py:117
  499.1 99.8 %collective-permute-start.66 = (bf16[4,160,640]{2,1,0:T(8,128)(2,1)}, bf16[4,160,640]{2,1,0:T(8,128)(2,1)}, u32[]{:S(2)}, u32[]{:S(2)}) collective-permute-start(bf16[4,160,640]{2,1,0:T(8,128)(2,1)} %dynamic-slice_bitcast_fusion.2), channel_id=1, source_target_pairs={{0,16},{16,0},{1,17},{17,1},{2,18},{18,2},{3,19},{19,3},{4,20},{20... | collective-permute-start | bytes 2457608 | tf_op jit(solution)/shard_map/ppermute | solution.py:117
  503.2 97.8 %collective-permute-start.55 = (bf16[2,4,40,1280]{3,2,0,1:T(8,128)(2,1)}, bf16[2,4,40,1280]{3,2,0,1:T(8,128)(2,1)}, u32[]{:S(2)}, u32[]{:S(2)}) collective-permute-start(bf16[2,4,40,1280]{3,2,0,1:T(8,128)(2,1)} %dynamic-slice_bitcast_fusion.4), channel_id=1, source_target_pairs={{0,16},{16,0},{1,17},{17,1},{2,18},{18,2},{3,19},{19,3},{4,20},{20... | collective-permute-start | bytes 2457608 | tf_op jit(solution)/shard_map/ppermute | solution.py:117
  593.9 140.7 %collective-permute-start.30 = (bf16[2,2,4,40,960]{4,3,1,2,0:T(8,128)(2,1)}, bf16[2,2,4,40,960]{4,3,1,2,0:T(8,128)(2,1)}, u32[]{:S(2)}, u32[]{:S(2)}) collective-permute-start(bf16[2,2,4,40,960]{4,3,1,2,0:T(8,128)(2,1)} %bitcast.336), channel_id=1, source_target_pairs={{0,8},{8,0},{1,9},{9,1},{2,10},{10,2},{3,11},{11,3},{4,12},{12,4},... | collective-permute-start | bytes 3686408 | tf_op jit(solution)/shard_map/ppermute | solution.py:117
  595.9 143.2 %collective-permute-start.25 = (bf16[2,2,4,40,960]{4,3,1,2,0:T(8,128)(2,1)}, bf16[2,2,4,40,960]{4,3,1,2,0:T(8,128)(2,1)S(1)}, u32[]{:S(2)}, u32[]{:S(2)}) collective-permute-start(bf16[2,2,4,40,960]{4,3,1,2,0:T(8,128)(2,1)} %bitcast.337), channel_id=1, source_target_pairs={{0,16},{16,0},{1,17},{17,1},{2,18},{18,2},{3,19},{19,3},{4,20},{20... | collective-permute-start | bytes 3686408 | tf_op jit(solution)/shard_map/ppermute | solution.py:117
  730.8 101.3 %collective-permute-start.12 = (bf16[128,1280]{1,0:T(8,128)(2,1)}, bf16[128,1280]{1,0:T(8,128)(2,1)}, u32[]{:S(2)}, u32[]{:S(2)}) collective-permute-start(bf16[128,1280]{1,0:T(8,128)(2,1)} %get-tuple-element.64), channel_id=1, source_target_pairs={{5,0},{0,1},{1,2},{4,3},{7,4},{2,5},{3,6},{6,7},{13,8},{8,9},{9,10... | collective-permute-start | bytes 983048 | tf_op jit(solution)/shard_map/ppermute | solution.py:100
  (124 other events, 2050.5 us)
Sparse Core Ops, SparseCore 0:
  10.8 98.6 all-gather.5
  112.3 61.8 all-gather.7
  177.0 96.3 all-gather.9
  276.0 94.4 all-gather.11

commit v2 on v1

--- a/solution.py
+++ b/solution.py
@@ -121,82 +121,86 @@
     return total.astype(values.dtype)
 
 
-def reduce_chips(values, seq_axis):
-    half = values.shape[-1] // 2
-    first = reduce_axis(reduce_axis(values[..., :half], 0, "ya"), 0, "xb")
-    second = reduce_axis(reduce_axis(values[..., half:], 1, "xb"), 0, "ya")
-    first = reduce_axis(first, seq_axis, "seq")
-    second = reduce_axis(second, seq_axis, "seq")
-    return jnp.concatenate([first, second], axis=-1)
-
-
-def reduce_columns(grad, parts):
+def reduce_near(first, second):
+    first = reduce_axis(reduce_axis(first, 0, "ya"), 0, "xb")
+    second = reduce_axis(reduce_axis(second, 1, "xb"), 0, "ya")
+    return [first, second]
+
+
+def reduce_far(halves):
+    return [reduce_axis(half, 0, "seq") for half in halves]
+
+
+def columns_near(grad):
     ya, xb, chips = size("ya"), size("xb"), size("seq")
     rows = grad.shape[0] // (ya * xb * 2 * chips)
-    core = lax.axis_index("core")
-    done = reduce_chips(grad.reshape(ya, xb, 2, chips, rows, -1), 1)
-    own = pick(done, 0, core).reshape(rows, parts, 1, -1)
-    other = swap(pick(done, 0, 1 - core)).reshape(rows, parts, 1, -1)
-    return by_core(own, other, 2).reshape(rows, -1).astype(F32)
+    grad = grad.reshape(ya, xb, 2, chips, rows, -1)
+    return reduce_near(grad[:, :, 0], grad[:, :, 1])
+
+
+def columns_own(halves, parts):
+    rows = halves[0].shape[0]
+    first = lax.axis_index("core") == 0
+    own = jnp.where(first, halves[0], halves[1]).reshape(rows, parts, 1, -1)
+    other = swap(jnp.where(first, halves[1], halves[0])).reshape(rows, parts, 1, -1)
+    return by_core(own, other, 2).astype(F32)
 
 
 def forward_kernel(q_ref, k_ref, v_ref, mask_ref, o_ref, lse_ref):
     rows, lanes = q_ref.shape
     dim = lanes // 2
     scale = dim ** (-0.5)
-    valid = mask_ref[...] > 0
-    for head in range(2):
-        part = slice(head * dim, (head + 1) * dim)
-        keys = k_ref[:, part]
-        turned = v_ref[:, part].T
-
-        def block(index, carry):
-            start = pl.multiple_of(index * QB, QB)
+    parts = [slice(head * dim, (head + 1) * dim) for head in range(2)]
+    turned = [v_ref[:, part].T for part in parts]
+
+    def block(index, carry):
+        start = pl.multiple_of(index * QB, QB)
+        valid = mask_ref[...] > 0
+        for head, part in enumerate(parts):
             queries = q_ref[pl.ds(start, QB), part] * BF(scale)
-            scores = jnp.where(valid, dot(keys, queries, NT), NEG)
+            scores = jnp.where(valid, dot(k_ref[:, part], queries, NT), NEG)
             top = jnp.max(scores, axis=0, keepdims=True)
             exponent = jnp.exp(scores - top)
             total = jnp.sum(exponent, axis=0, keepdims=True)
-            mixed = dot(turned, exponent.astype(BF), NN) / total
+            mixed = dot(turned[head], exponent.astype(BF), NN) / total
             o_ref[pl.ds(start, QB), part] = mixed.T.astype(BF)
             lse_ref[0, head : head + 1, pl.ds(start, QB)] = top + jnp.log(total)
-            return carry
-
-        lax.fori_loop(0, rows // QB, block, 0)
+        return carry
+
+    lax.fori_loop(0, rows // QB, block, 0)
 
 
 def backward_kernel(q_ref, k_ref, v_ref, d_ref, lse_ref, mask_ref, out_ref, dk_ref, dv_ref):
     rows, lanes = q_ref.shape
     dim = lanes // 2
     scale = dim ** (-0.5)
-    valid = mask_ref[...] > 0
-    for head in range(2):
-        part = slice(head * dim, (head + 1) * dim)
-        keys = k_ref[:, part]
-        values = v_ref[:, part]
-        turned = keys.T
-        dk_ref[...] = jnp.zeros_like(dk_ref)
-        dv_ref[...] = jnp.zeros_like(dv_ref)
-
-        def block(index, carry):
-            start = pl.multiple_of(index * QB, QB)
+    parts = [slice(head * dim, (head + 1) * dim) for head in range(2)]
+    turned = [k_ref[:, part].T for part in parts]
+    dk_ref[...] = jnp.zeros_like(dk_ref)
+    dv_ref[...] = jnp.zeros_like(dv_ref)
+
+    def block(index, carry):
+        start = pl.multiple_of(index * QB, QB)
+        valid = mask_ref[...] > 0
+        for head, part in enumerate(parts):
             queries = q_ref[pl.ds(start, QB), part] * BF(scale)
             incoming = d_ref[pl.ds(start, QB), part]
             lse = lse_ref[0, head : head + 1, pl.ds(start, QB)]
-            scores = jnp.where(valid, dot(keys, queries, NT), NEG)
+            scores = jnp.where(valid, dot(k_ref[:, part], queries, NT), NEG)
             soft = jnp.exp(scores - lse)
-            d_soft = dot(values, incoming, NT)
+            d_soft = dot(v_ref[:, part], incoming, NT)
             inner = jnp.sum(soft * d_soft, axis=0, keepdims=True)
             d_scores = (soft * (d_soft - inner)).astype(BF)
-            dv_ref[...] += dot(soft.astype(BF), incoming, NN)
-            dk_ref[...] += dot(d_scores, queries, NN)
-            d_queries = dot(turned, d_scores, NN) * scale
+            dv_ref[head] += dot(soft.astype(BF), incoming, NN)
+            dk_ref[head] += dot(d_scores, queries, NN)
+            d_queries = dot(turned[head], d_scores, NN) * scale
             out_ref[0, pl.ds(start, QB), part] = d_queries.T.astype(BF)
-            return carry
-
-        lax.fori_loop(0, rows // QB, block, 0)
-        out_ref[1, :, part] = dk_ref[...].astype(BF)
-        out_ref[2, :, part] = dv_ref[...].astype(BF)
+        return carry
+
+    lax.fori_loop(0, rows // QB, block, 0)
+    for head, part in enumerate(parts):
+        out_ref[1, :, part] = dk_ref[head].astype(BF)
+        out_ref[2, :, part] = dv_ref[head].astype(BF)
 
 
 def attend(project, mask):
@@ -229,31 +233,119 @@
     )(project, project, project, mask)
 
 
-def attend_back(project, incoming, lse, mask):
+def attend_back(project, incoming, lse, mask, first, count):
     rows, columns = project.shape
-    width = columns // 3
     pair = 2 * 64
-    pairs = width // pair
+    pairs = columns // (3 * pair)
+    width = count * pair
     cost = pl.CostEstimate(
         flops=10 * rows * rows * width, bytes_accessed=14 * rows * width, transcendentals=0
     )
     return pl.pallas_call(
         backward_kernel,
-        grid=(pairs,),
+        grid=(count,),
         in_specs=[
-            pl.BlockSpec((rows, pair), lambda j: (0, j)),
-            pl.BlockSpec((rows, pair), lambda j: (0, pairs + j)),
-            pl.BlockSpec((rows, pair), lambda j: (0, 2 * pairs + j)),
-            pl.BlockSpec((rows, pair), lambda j: (0, j)),
-            pl.BlockSpec((1, 2, rows), lambda j: (j, 0, 0)),
+            pl.BlockSpec((rows, pair), lambda j: (0, first + j)),
+            pl.BlockSpec((rows, pair), lambda j: (0, pairs + first + j)),
+            pl.BlockSpec((rows, pair), lambda j: (0, 2 * pairs + first + j)),
+            pl.BlockSpec((rows, pair), lambda j: (0, first + j)),
+            pl.BlockSpec((1, 2, rows), lambda j: (first + j, 0, 0)),
             pl.BlockSpec((rows, QB), lambda j: (0, 0)),
         ],
         out_specs=pl.BlockSpec((3, rows, pair), lambda j: (0, 0, j)),
         out_shape=jax.ShapeDtypeStruct((3, rows, width), BF),
-        scratch_shapes=[pltpu.VMEM((rows, pair // 2), F32), pltpu.VMEM((rows, pair // 2), F32)],
+        scratch_shapes=[pltpu.VMEM((2, rows, pair // 2), F32), pltpu.VMEM((2, rows, pair // 2), F32)],
         cost_estimate=cost,
         name="attend_back",
     )(project, project, project, incoming, lse, mask)
+
+
+def gather_axis(values, name):
+    count = size(name)
+    index = lax.axis_index(name)
+    if count > 4:
+        return lax.all_gather(values, name, axis=0, tiled=False)
+    result = jnp.zeros((count,) + values.shape, values.dtype)
+    result = lax.dynamic_update_slice_in_dim(result, values[None], index, 0)
+    for step in range(1, count):
+        part = lax.ppermute(values, name, [(j, (j + step) % count) for j in range(count)])
+        slot = (index - step + count) % count
+        result = lax.dynamic_update_slice_in_dim(result, part[None], slot, 0)
+    return result
+
+
+def relative(values, name):
+    count = size(name)
+    parts = [values]
+    for step in range(1, count):
+        parts.append(lax.ppermute(values, name, [(j, (j + step) % count) for j in range(count)]))
+    return parts
+
+
+def lay_kernel(slots_ref, *refs):
+    out_ref = refs[-1]
+    side = len(out_ref.shape) == 3
+    width = refs[0].shape[1]
+    for index in range((len(refs) - 1) // 2):
+
+        @pl.when(pl.program_id(0) == index)
+        def _():
+            if side:
+                out_ref[0, :, :width] = refs[2 * index][...]
+                out_ref[0, :, width:] = refs[2 * index + 1][...]
+            else:
+                out_ref[0, 0] = refs[2 * index][...]
+                out_ref[0, 1] = refs[2 * index + 1][...]
+
+
+def lay(first, second, slots, side):
+    count = len(first)
+    rows, width = first[0].shape
+    block = (rows, 2 * width) if side else (2, rows, width)
+    rest = (0,) * len(block)
+    pieces = [piece for pair in zip(first, second) for piece in pair]
+    whole = pl.BlockSpec((rows, width), lambda j, slots: (0, 0), pipeline_mode=pl.Buffered(1))
+    return pl.pallas_call(
+        lay_kernel,
+        grid_spec=pltpu.PrefetchScalarGridSpec(
+            num_scalar_prefetch=1,
+            grid=(count,),
+            in_specs=[whole] * (2 * count),
+            out_specs=pl.BlockSpec((1,) + block, lambda j, slots: (slots[j],) + rest),
+        ),
+        out_shape=jax.ShapeDtypeStruct((count,) + block, first[0].dtype),
+        cost_estimate=pl.CostEstimate(
+            flops=0, bytes_accessed=8 * count * rows * width, transcendentals=0
+        ),
+        name="lay",
+    )(slots, *pieces)
+
+
+def gather_seq(values):
+    done = gather_axis(values, "seq")
+    chips, _, rows, width = done.shape
+    return [done[:, half].reshape(chips * rows, width) for half in range(2)]
+
+
+def gather_chips(halves, side=False):
+    ya, xb = size("ya"), size("xb")
+    ia, ib = lax.axis_index("ya"), lax.axis_index("xb")
+    first = {}
+    for b, part in enumerate(relative(halves[0], "xb")):
+        for a, piece in enumerate(relative(part, "ya")):
+            first[a, b] = piece
+    second = {}
+    for a, part in enumerate(relative(halves[1], "ya")):
+        for b, piece in enumerate(relative(part, "xb")):
+            second[a, b] = piece
+    keys = sorted(first)
+    slots = jnp.stack([((ia - a + ya) % ya) * xb + (ib - b + xb) % xb for a, b in keys])
+    slots = slots.astype(jnp.int32)
+    return lay([first[key] for key in keys], [second[key] for key in keys], slots, side)
+
+
+def after(values, *others):
+    return lax.optimization_barrier((values,) + others)[0]
 
 
 def body(tokens, lengths, cotangent, w_qkv, w_out, w_up, w_down, *small):
@@ -265,7 +357,8 @@
     own_rows = chips * rows_local // 2
     sizes = [member.shape[0] for member in small]
 
-    packed = lax.all_gather(jnp.concatenate(small)[None], ALL, axis=0, tiled=True)
+    packed = gather_axis(gather_axis(gather_axis(gather_axis(jnp.concatenate(small), "seq"), "core"), "xb"), "ya")
+    packed = packed.reshape(-1, sum(sizes))
     vectors, at = [], 0
     for count in sizes:
         vectors.append(packed[:, at : at + count].reshape(-1).astype(F32))
@@ -274,13 +367,28 @@
         gain_one, shift_one, bias_query, bias_value, bias_out,
         gain_two, shift_two, bias_up, bias_down,
     ) = vectors
-    full_qkv = lax.all_gather(w_qkv, ALL, axis=0, tiled=True)
-    qkv = pick(full_qkv.reshape(width, 3, 2, half), 2, core).reshape(width, 3 * half)
-    out_full = lax.all_gather(w_out, ALL, axis=0, tiled=True)
-    full_up = lax.all_gather(w_up, ALL, axis=0, tiled=True)
-    hidden_all = full_up.shape[1]
-    up = pick(full_up.reshape(width, chip_pairs, 2, -1), 2, core).reshape(width, hidden_all // 2)
-    down = lax.all_gather(w_down, ("ya", "xb", "seq"), axis=0, tiled=True)
+    def columns(shard, parts):
+        pieces = shard.reshape(shard.shape[0], parts, 2, -1)
+        own = pick(pieces, 2, core).reshape(shard.shape[0], -1)
+        other = swap(pick(pieces, 2, 1 - core).reshape(shard.shape[0], -1))
+        return jnp.where(core == 0, jnp.stack([own, other]), jnp.stack([other, own]))
+
+    hidden_half = w_up.shape[1] // 2
+    inputs = to_cells(tokens)
+    seq_qkv = gather_seq(columns(w_qkv, 3))
+    seq_out = gather_seq(columns(w_out, 1))
+    seq_up = gather_seq(after(columns(w_up, chip_pairs), seq_qkv[0]))
+    shards = after(w_down, seq_up[0])
+    seq_down = gather_seq(jnp.stack([shards[:, :half], shards[:, half:]]))
+    incoming = to_cells(after(cotangent, seq_up[0]))
+    qkv = gather_chips(seq_qkv).reshape(width, 3 * half)
+    seq_out = after(seq_out, qkv)
+    out_own = gather_chips(seq_out).reshape(width, half)
+    out_other = swap(out_own)
+    seq_up = after(seq_up, qkv)
+    up = gather_chips(seq_up).reshape(width, hidden_half)
+    seq_down = after(seq_down, up)
+    down = gather_chips(seq_down, True).reshape(hidden_half, width)
     up_bias = pick(bias_up.reshape(chip_pairs, 2, -1), 1, core).reshape(-1)
     project_bias = jnp.concatenate(
         [
@@ -290,8 +398,6 @@
         ]
     )
 
-    inputs = to_cells(tokens)
-    incoming = to_cells(cotangent)
     other_counts = swap(lengths)
     counts = jnp.where(core == 0, jnp.concatenate([lengths, other_counts]), jnp.concatenate([other_counts, lengths]))
     count = lax.dynamic_index_in_dim(counts, place, 0, keepdims=False)
@@ -308,7 +414,8 @@
     project = (dot(normed_all, qkv, NN) + project_bias).astype(BF)
     mixed_heads, lse = attend(project, mask)
     mixed_own = by_core(mixed_heads[:own_rows], swap(mixed_heads[own_rows:]), 1)
-    middle = inputs + (dot(mixed_own, out_full, NN) + bias_out)
+    attended = by_core(dot(mixed_own, out_own, NN), dot(mixed_own, out_other, NN), 1)
+    middle = inputs + (attended + bias_out)
     normal_two, inverse_two = normalise(middle)
     second_low = (normal_two * gain_two + shift_two).astype(BF)
     second_all = jnp.concatenate([second_low, swap(second_low)], axis=0)
@@ -316,17 +423,20 @@
     half_erf = 0.5 * (1.0 + lax.erf(hidden * (0.5**0.5)))
     active = (hidden * half_erf).astype(BF)
     slope = (half_erf + hidden * jnp.exp(-0.5 * hidden * hidden) * 0.3989422804014327).astype(BF)
+    incoming_all = jnp.concatenate([incoming, swap(incoming)], axis=0)
+    grad_down = dot(active, incoming_all, TN, BF)
+    active = after(active, grad_down)
+    grad_down = grad_down.reshape(ya, xb, chips, -1, width)
+    near_down = reduce_near(grad_down[..., :half], grad_down[..., half:])
+    far_down = reduce_far(near_down)
     branch_own = dot(active[:own_rows], down, NN)
     branch_other = swap(dot(active[own_rows:], down, NN).astype(BF))
     output = (middle + (branch_own + branch_other.astype(F32) + bias_down)).astype(BF)
     output = from_cells(output, cells)
 
-    incoming_all = jnp.concatenate([incoming, swap(incoming)], axis=0)
     grad_bias_down = jnp.sum(incoming.astype(F32), axis=0)
     d_hidden = (dot(incoming_all, down, NT) * slope.astype(F32)).astype(BF)
-    grad_down = dot(active, incoming_all, TN, BF)
-    grad_down = reduce_chips(grad_down.reshape(ya, xb, chips, -1, width), 0).astype(F32)
-    grad_up = reduce_columns(dot(second_all, d_hidden, TN, BF), chip_pairs)
+    near_up = columns_near(dot(second_all, d_hidden, TN, BF))
     grad_bias_up = jnp.sum(d_hidden.astype(F32), axis=0)
     d_second = dot(d_hidden[:own_rows], up, NT) + swap(
         dot(d_hidden[own_rows:], up, NT).astype(BF)
@@ -336,25 +446,42 @@
     grad_shift_two = jnp.sum(d_second, axis=0)
     d_attend = d_middle.astype(BF)
     grad_bias_out = jnp.sum(d_attend.astype(F32), axis=0)
-    d_mixed = dot(d_attend, out_full, NT).astype(BF)
+    low, high = d_attend[:, :half], d_attend[:, half:]
+    d_attend_own = jnp.where(core == 0, low, high)
+    d_attend_other = jnp.where(core == 0, high, low)
+    d_mixed = (dot(d_attend_own, out_own, NT) + dot(d_attend_other, out_other, NT)).astype(BF)
     low, high = d_mixed[:, :half], d_mixed[:, half:]
     d_mixed_heads = jnp.concatenate(
         [jnp.where(core == 0, low, high), swap(jnp.where(core == 0, high, low))], axis=0
     )
-    d_project = attend_back(project, d_mixed_heads, lse, mask)
-
-    low, high = d_attend[:, :half], d_attend[:, half:]
-    d_attend_columns = jnp.concatenate(
-        [jnp.where(core == 0, low, high), swap(jnp.where(core == 0, high, low))], axis=0
-    )
+
+    d_attend_columns = jnp.concatenate([d_attend_own, swap(d_attend_other)], axis=0)
     mixed_other = by_core(mixed_heads[own_rows:], swap(mixed_heads[:own_rows]), 1)
     mixed_all = jnp.concatenate([mixed_own, mixed_other], axis=0)
-    grad_out = reduce_columns(dot(mixed_all, d_attend_columns, TN, BF), 1)
-
+    near_out = columns_near(dot(mixed_all, d_attend_columns, TN, BF))
+
+    pairs = half // 128
+    front = (pairs + 1) // 2
+    d_mixed_heads = after(d_mixed_heads, far_down)
+    part = attend_back(project, d_mixed_heads, lse, mask, 0, front)
+    flats = [jnp.concatenate([part[0], part[1], part[2]], axis=1)]
+    far_up = reduce_far(near_up)
+    near_qkv = [columns_near(dot(normed_all, flats[0], TN, BF))]
+    d_mixed_heads = after(d_mixed_heads, near_up, near_out, flats[0])
+    part_two = attend_back(project, d_mixed_heads, lse, mask, front, pairs - front)
+    flats.append(jnp.concatenate([part_two[0], part_two[1], part_two[2]], axis=1))
+    near_qkv.append(columns_near(dot(normed_all, flats[1], TN, BF)))
+    far_out = reduce_far(near_out)
+
+    d_project = jnp.concatenate([part, part_two], axis=2)
     sides = jnp.sum(d_project.astype(F32), axis=1)
     flat = jnp.concatenate([d_project[0], d_project[1], d_project[2]], axis=1)
     d_normed = dot(flat[:own_rows], qkv, NT) + swap(dot(flat[own_rows:], qkv, NT).astype(BF)).astype(F32)
-    grad_qkv = reduce_columns(dot(normed_all, flat, TN, BF), 3)
+    grad_down = jnp.concatenate(far_down, axis=-1).astype(F32)
+    grad_up = columns_own(far_up, chip_pairs).reshape(w_up.shape)
+    grad_out = columns_own(far_out, 1).reshape(w_out.shape)
+    grad_qkv = [columns_own(reduce_far(near), 3) for near in near_qkv]
+    grad_qkv = jnp.concatenate(grad_qkv, axis=-1).reshape(w_qkv.shape)
     input_grad = d_middle + norm_back(normal_one, inverse_one, d_normed, gain_one)
     input_grad = from_cells(input_grad.astype(BF), cells).astype(F32)
     grad_gain_one = jnp.sum(d_normed * normal_one, axis=0)

time: 853 us -> 856 us (level); the launches traced: 847 us -> 839 us
  blocking collectives: 68.9 us -> 0 us
  starting transfers between devices: 133 us -> 199 us
  local copies, waits for them, and re-layouts: 104 us -> 78.9 us
  Pallas kernels: 92.5 us -> 110 us
  between operations: 15.8 us -> 3.47 us
  other arithmetic: 43.6 us -> 53.8 us
    ppermute x0 -> x42, waiting for transfers between devices: none -> 142 us  [the longest x24 73.2 us: relative(): lax.ppermute(values, name, [(j, (j + step) % count) for j in range(count)])]
    all_gather x4 -> x0, waiting for transfers between devices: 141 us -> none  [the longest x1 73.4 us: body(): full_up = lax.all_gather(w_up, ALL, axis=0, tiled=True)]
    unnamed x1 -> x0, blocking collectives: 68.9 us -> none
    ppermute x0 -> x42, starting transfers between devices: none -> 61.7 us  [the longest x18 34.1 us: gather_axis(): lax.ppermute(values, name, [(j, (j + step) % count) for j in range(count)])]
    ppermute x46 -> x56, waiting for transfers between devices: 130 us -> 95.5 us  [reduce_axis(): parts.append(lax.ppermute(piece, name, pairs))]
    all_gather x3 -> x0, local copies, waits for them, and re-layouts: 31.5 us -> none  [the longest x1 17.7 us: body(): full_up = lax.all_gather(w_up, ALL, axis=0, tiled=True)]
    pallas_call x1 -> x6, Pallas kernels: 50.2 us -> 71 us  [the longest x2 47.6 us: attend_back(): pl.pallas_call(backward_kernel, grid=(count,), in_specs=[pl.BlockSpec((ro...]
    ppermute x8, waiting for transfers between devices: 4.91 us -> 25.6 us  [from_cells(): parts.append(lax.ppermute(piece, ('core', 'seq'), back))]
  transfers between devices with their start and end apart: 80 -> 133, of which waited for: 26 -> 45; matrix products, arithmetic and copies ran while one was open for 27% -> 25% of each run, Pallas kernels for 11% -> 13%
where the time goes in v2:
time: 856 us; the launch traced here: 839 us
  waiting for transfers between devices  274 us (32%)
  starting transfers between devices  199 us (23%)
  matrix products  120 us (14%)
  Pallas kernels  110 us (13%)
  local copies, waits for them, and re-layouts  78.9 us (9%)
  other arithmetic  53.8 us (6%)
    dot_general x18, matrix products, dot(): lax.dot_general(left, right, (dims, ((), ())), preferred_element_type=out)  120 us
    ppermute x56, waiting for transfers between devices, reduce_axis(): parts.append(lax.ppermute(piece, name, pairs))  95.5 us
    ppermute x56, starting transfers between devices, reduce_axis(): parts.append(lax.ppermute(piece, name, pairs))  90.5 us
    ppermute x24, waiting for transfers between devices, relative(): lax.ppermute(values, name, [(j, (j + step) % count) for j in range(count)])  73.2 us
    ppermute x18, waiting for transfers between devices, gather_axis(): lax.ppermute(values, name, [(j, (j + step) % count) for j in range(count)])  69 us
    pallas_call x2, Pallas kernels, attend_back(): pl.pallas_call(backward_kernel, grid=(count,), in_specs=[pl.BlockSpec((ro...  47.6 us
    pallas_call x1, Pallas kernels, attend(): pl.pallas_call(forward_kernel, grid=(pairs,), in_specs=[pl.BlockSpec((row...  39.2 us
    ppermute x18, starting transfers between devices, gather_axis(): lax.ppermute(values, name, [(j, (j + step) % count) for j in range(count)])  34.1 us
  transfers between devices with their start and end apart: 133, of which 45 were waited for; matrix products, arithmetic and copies ran while one was open for 25% of the time, Pallas kernels for 13%

profile of v2, /device:TPU:0, one launch (start us, length us, event | category | flops | bytes accessed | tf_op | source)
XLA Modules:
  0.0 838.9 jit_solution(17733408867322981151)
XLA Ops:
  95.1 15.9 %collective-permute-done.13 = bf16[2,40,1920]{2,1,0:T(8,128)(2,1)S(1)} collective-permute-done((bf16[2,40,1920]{2,1,0:T(8,128)(2,1)S(1)}, bf16[2,40,1920]{2,1,0:T(8,128)(2,1)S(1)}, u32[]{:S(2)}, u32[]{:S(2)}) %collective-permute-start.13) | collective-permute-done | bytes 307232 | tf_op jit(solution)/shard_map/ppermute | solution.py:271
  127.1 15.1 %collective-permute-done.37 = bf16[2,40,2560]{2,1,0:T(8,128)(2,1)S(1)} collective-permute-done((bf16[2,40,2560]{2,1,0:T(8,128)(2,1)S(1)}, bf16[2,40,2560]{2,1,0:T(8,128)(2,1)S(1)}, u32[]{:S(2)}, u32[]{:S(2)}) %collective-permute-start.37) | collective-permute-done | bytes 409632 | tf_op jit(solution)/shard_map/ppermute | solution.py:271
  145.1 9.2 %collective-permute-start.46 = (bf16[128,1280]{1,0:T(8,128)(2,1)S(1)}, bf16[128,1280]{1,0:T(8,128)(2,1)S(1)}, u32[]{:S(2)}, u32[]{:S(2)}) collective-permute-start(bf16[128,1280]{1,0:T(8,128)(2,1)S(1)} %get-tuple-element.109), channel_id=1, source_target_pairs={{0,1},{1,4},{2,5},{3,0},{4,3},{5,6},{6,7},{7,2},{8,9},{9,12},{10,1... | collective-permute-start | bytes 983048 | tf_op jit(solution)/shard_map/ppermute | solution.py:80
  159.1 8.5 %collective-permute-done.46 = bf16[128,1280]{1,0:T(8,128)(2,1)S(1)} collective-permute-done((bf16[128,1280]{1,0:T(8,128)(2,1)S(1)}, bf16[128,1280]{1,0:T(8,128)(2,1)S(1)}, u32[]{:S(2)}, u32[]{:S(2)}) %collective-permute-start.46) | collective-permute-done | bytes 327712 | tf_op jit(solution)/shard_map/ppermute | solution.py:80
  176.1 8.8 %collective-permute-done.19.refs_6_ = bf16[160,1920]{1,0:T(8,128)(2,1)S(1)} collective-permute-done((bf16[160,1920]{1,0:T(8,128)(2,1)S(1)}, bf16[160,1920]{1,0:T(8,128)(2,1)S(1)}, u32[]{:S(2)}, u32[]{:S(2)}) %collective-permute-start.19) | collective-permute-done | bytes 614432 | tf_op jit(solution)/shard_map/ppermute | solution.py:281
  195.1 10.7 %add_convert_fusion.q_ref.k_ref.v_ref = bf16[1024,1920]{1,0:T(8,128)(2,1)} fusion(f32[1920]{0:T(1024)S(1)} %copy-done.77, bf16[1280,1920]{1,0:T(8,128)(2,1)} %bitcast.572, bf16[512,1280]{1,0:T(8,128)(2,1)} %collective-permute-done.10, bf16[512,1280]{1,0:T(8,128)(2,1)} %fusion.31), kind=kOutput, calls=%fused_computation.11 | convolution fusion | flops 5042339840 | bytes 11476480 | tf_op jit(solution)/shard_map/dot_general | solution.py:20
  209.5 39.2 %attend.1 = (bf16[1024,640]{1,0:T(8,128)(2,1)}, f32[5,2,1024]{2,1,0:T(2,128)}) custom-call(bf16[1024,1920]{1,0:T(8,128)(2,1)} %add_convert_fusion.q_ref.k_ref.v_ref, bf16[1024,1920]{1,0:T(8,128)(2,1)} %add_convert_fusion.q_ref.k_ref.v_ref, bf16[1024,1920]{1,0:T(8,128)(2,1)} %add_convert_fusion.q_ref.k_ref.v_ref, f32[1024,256]{1,0:T(8,128)} %broadcast_in_dim.207.mask_ref), custom_call_target="tpu_custom_call" | custom-call | flops 2684354560 | bytes 5242880 | tf_op jit(solution)/shard_map/attend/pallas_call | solution.py:214
  279.0 11.8 %collective-permute-done.40.refs_3_ = bf16[160,2560]{1,0:T(8,128)(2,1)S(1)} collective-permute-done((bf16[160,2560]{1,0:T(8,128)(2,1)S(1)}, bf16[160,2560]{1,0:T(8,128)(2,1)S(1)}, u32[]{:S(2)}, u32[]{:S(2)}) %collective-permute-start.40) | collective-permute-done | bytes 819232 | tf_op jit(solution)/shard_map/ppermute | solution.py:281
  293.2 14.3 %collective-permute-done.43.refs_6_ = bf16[160,2560]{1,0:T(8,128)(2,1)} collective-permute-done((bf16[160,2560]{1,0:T(8,128)(2,1)}, bf16[160,2560]{1,0:T(8,128)(2,1)}, u32[]{:S(2)}, u32[]{:S(2)}) %collective-permute-start.43) | collective-permute-done | bytes 819232 | tf_op jit(solution)/shard_map/ppermute | solution.py:281
  326.4 9.3 %collective-permute-done.53.refs_2_ = bf16[640,640]{1,0:T(8,128)(2,1)} collective-permute-done((bf16[640,640]{1,0:T(8,128)(2,1)}, bf16[640,640]{1,0:T(8,128)(2,1)}, u32[]{:S(2)}, u32[]{:S(2)}) %collective-permute-start.53) | collective-permute-done | bytes 819232 | tf_op jit(solution)/shard_map/ppermute | solution.py:281
  343.5 9.7 %collective-permute-done.54.refs_3_ = bf16[640,640]{1,0:T(8,128)(2,1)} collective-permute-done((bf16[640,640]{1,0:T(8,128)(2,1)S(1)}, bf16[640,640]{1,0:T(8,128)(2,1)}, u32[]{:S(2)}, u32[]{:S(2)}) %collective-permute-start.54) | collective-permute-done | bytes 819232 | tf_op jit(solution)/shard_map/ppermute | solution.py:281
  354.7 16.8 %collective-permute-done.57.refs_6_ = bf16[640,640]{1,0:T(8,128)(2,1)} collective-permute-done((bf16[640,640]{1,0:T(8,128)(2,1)}, bf16[640,640]{1,0:T(8,128)(2,1)}, u32[]{:S(2)}, u32[]{:S(2)}) %collective-permute-start.57) | collective-permute-done | bytes 819232 | tf_op jit(solution)/shard_map/ppermute | solution.py:281
  378.3 13.4 %multiply_convert_fusion.1 = (bf16[1024,2560]{1,0:T(8,128)(2,1)}, f32[1024,2560]{1,0:T(8,128)}) fusion(f32[2560]{0:T(1024)S(1)} %copy-done.75, bf16[1280,2560]{1,0:T(8,128)(2,1)} %bitcast.552, bf16[512,1280]{1,0:T(8,128)(2,1)} %collective-permute-done.34, bf16[512,1280]{1,0:T(8,128)(2,1)} %get-tuple-element.70), kind=kOutput, calls=%fused_computation.8 | convolution fusion | flops 6731857920 | bytes 24913920 | tf_op jit(solution)/shard_map/dot_general | solution.py:20
  391.8 13.2 %convert_reduce_fusion = (f32[2560]{0:T(1024)S(1)}, bf16[1024,2560]{1,0:T(8,128)(2,1)}) fusion(f32[1024,2560]{1,0:T(8,128)} %get-tuple-element.186, f32[2560]{0:T(1024)S(1)} %copy-done.75, bf16[2560,1280]{1,0:T(8,128)(2,1)S(1)} %bitcast.558, bf16[512,1280]{1,0:T(8,128)(2,1)S(1)} %collective-permute-done.49, bf16[512,1280]{1,0:T(8,128)(2,1)S(1)} %bitcast.546), kind=kOutput, calls=%fused_computation.6 | convolution fusion | flops 6755448320 | bytes 24924160 | tf_op jit(solution)/shard_map/dot_general | solution.py:20
  411.6 9.2 %fusion.43 = bf16[1280,2560]{1,0:T(8,128)(2,1)S(1)} fusion(bf16[1024,2560]{1,0:T(8,128)(2,1)S(1)} %copy-done.79, bf16[512,1280]{1,0:T(8,128)(2,1)} %collective-permute-done.34, bf16[512,1280]{1,0:T(8,128)(2,1)} %get-tuple-element.70), kind=kOutput, calls=%fused_computation.88 | convolution fusion | flops 6716129280 | bytes 14417920 | tf_op jit(solution)/shard_map/dot_general | solution.py:20
  446.8 8.4 multiply_reduce_fusion
  517.2 14.4 %collective-permute-done.84 = bf16[2,4,40,640]{3,2,1,0:T(8,128)(2,1)S(1)} collective-permute-done((bf16[2,4,40,640]{3,2,1,0:T(8,128)(2,1)S(1)}, bf16[2,4,40,640]{3,2,1,0:T(8,128)(2,1)S(1)}, u32[]{:S(2)}, u32[]{:S(2)}) %collective-permute-start.84) | collective-permute-done | bytes 409632 | tf_op jit(solution)/shard_map/ppermute | solution.py:117
  533.3 12.5 %collective-permute-done.82 = bf16[2,4,40,640]{3,2,1,0:T(8,128)(2,1)S(1)} collective-permute-done((bf16[2,4,40,640]{3,2,1,0:T(8,128)(2,1)S(1)}, bf16[2,4,40,640]{3,2,1,0:T(8,128)(2,1)S(1)}, u32[]{:S(2)}, u32[]{:S(2)}) %collective-permute-start.82) | collective-permute-done | bytes 409632 | tf_op jit(solution)/shard_map/ppermute | solution.py:117
  581.5 9.5 %collective-permute-done.74 = bf16[160,640]{1,0:T(8,128)(2,1)S(1)} collective-permute-done((bf16[160,640]{1,0:T(8,128)(2,1)S(1)}, bf16[160,640]{1,0:T(8,128)(2,1)S(1)}, u32[]{:S(2)}, u32[]{:S(2)}) %collective-permute-start.74) | collective-permute-done | bytes 204832 | tf_op jit(solution)/shard_map/ppermute | solution.py:117
  617.5 28.0 %attend_back.2 = bf16[3,1024,384]{2,1,0:T(8,128)(2,1)} custom-call(bf16[1024,1920]{1,0:T(8,128)(2,1)} %add_convert_fusion.q_ref.k_ref.v_ref, bf16[1024,1920]{1,0:T(8,128)(2,1)} %add_convert_fusion.q_ref.k_ref.v_ref, bf16[1024,1920]{1,0:T(8,128)(2,1)} %add_convert_fusion.q_ref.k_ref.v_ref, bf16[1024,640]{1,0:T(8,128)(2,1)} %pad_maximum_fusion.10.d_ref, ...), custom_call_target="tpu_custom_call" | custom-call | flops 4026531840 | bytes 5505024 | tf_op jit(solution)/shard_map/attend_back/pallas_call | solution.py:244
  645.5 19.6 %attend_back.3 = bf16[3,1024,256]{2,1,0:T(8,128)(2,1)} custom-call(bf16[1024,1920]{1,0:T(8,128)(2,1)} %add_convert_fusion.q_ref.k_ref.v_ref, bf16[1024,1920]{1,0:T(8,128)(2,1)} %add_convert_fusion.q_ref.k_ref.v_ref, bf16[1024,1920]{1,0:T(8,128)(2,1)} %add_convert_fusion.q_ref.k_ref.v_ref, bf16[1024,640]{1,0:T(8,128)(2,1)} %pad_maximum_fusion.10.d_ref, ...), custom_call_target="tpu_custom_call" | custom-call | flops 2684354560 | bytes 3670016 | tf_op jit(solution)/shard_map/attend_back/pallas_call | solution.py:244
  712.4 15.0 %collective-permute-done.107 = bf16[2,4,40,768]{3,2,1,0:T(8,128)(2,1)} collective-permute-done((bf16[2,4,40,768]{3,2,1,0:T(8,128)(2,1)}, bf16[2,4,40,768]{3,2,1,0:T(8,128)(2,1)}, u32[]{:S(2)}, u32[]{:S(2)}) %collective-permute-start.107) | collective-permute-done | bytes 491552 | tf_op jit(solution)/shard_map/ppermute | solution.py:117
  756.8 7.9 collective-permute-done.97
  788.4 8.3 fusion.37
  (692 shorter events, 506.6 us)
Async XLA Ops:
  17.5 52.7 %collective-permute-start.11 = (bf16[40,1920]{1,0:T(8,128)(2,1)}, bf16[40,1920]{1,0:T(8,128)(2,1)S(1)}, u32[]{:S(2)}, u32[]{:S(2)}) collective-permute-start(bf16[40,1920]{1,0:T(8,128)(2,1)} %bitcast.306), channel_id=1, source_target_pairs={{0,4},{4,0},{1,5},{5,1},{2,6},{6,2},{3,7},{7,3},{8,12},{12,8},{9,1... | collective-permute-start | bytes 460808 | tf_op jit(solution)/shard_map/ppermute | solution.py:33
  24.5 49.2 %collective-permute-start.35 = (bf16[40,2560]{1,0:T(8,128)(2,1)S(1)}, bf16[40,2560]{1,0:T(8,128)(2,1)S(1)}, u32[]{:S(2)}, u32[]{:S(2)}) collective-permute-start(bf16[40,2560]{1,0:T(8,128)(2,1)S(1)} %bitcast.609), channel_id=1, source_target_pairs={{0,4},{4,0},{1,5},{5,1},{2,6},{6,2},{3,7},{7,3},{8,12},{12,8},{9,1... | collective-permute-start | bytes 614408 | tf_op jit(solution)/shard_map/ppermute | solution.py:33
  29.2 44.6 %collective-permute-start = (bf16[128,1280]{1,0:T(8,128)(2,1)S(1)}, bf16[128,1280]{1,0:T(8,128)(2,1)S(1)}, u32[]{:S(2)}, u32[]{:S(2)}) collective-permute-start(bf16[128,1280]{1,0:T(8,128)(2,1)S(1)} %get-tuple-element.116), channel_id=1, source_target_pairs={{0,0},{1,1},{2,4},{3,5},{4,2},{5,3},{6,6},{7,7},{8,8},{9,9},{10,12... | collective-permute-start | bytes 983048 | tf_op jit(solution)/shard_map/ppermute | solution.py:80
  84.0 109.7 %collective-permute-start.10 = (bf16[512,1280]{1,0:T(8,128)(2,1)}, bf16[512,1280]{1,0:T(8,128)(2,1)}, u32[]{:S(2)}, u32[]{:S(2)}) collective-permute-start(bf16[512,1280]{1,0:T(8,128)(2,1)} %fusion.31), channel_id=1, source_target_pairs={{0,4},{4,0},{1,5},{5,1},{2,6},{6,2},{3,7},{7,3},{8,12},{12,8},{9,1... | collective-permute-start | bytes 3932168 | tf_op jit(solution)/shard_map/ppermute | solution.py:33
  169.9 87.4 %collective-permute-start.50 = (bf16[2,160,640]{2,1,0:T(8,128)(2,1)}, bf16[2,160,640]{2,1,0:T(8,128)(2,1)}, u32[]{:S(2)}, u32[]{:S(2)}) collective-permute-start(bf16[2,160,640]{2,1,0:T(8,128)(2,1)} %pad_maximum_fusion.14), channel_id=1, source_target_pairs={{0,1},{1,2},{2,3},{3,0},{4,5},{5,6},{6,7},{7,4},{8,9},{9,10},{10,1... | collective-permute-start | bytes 1228808 | tf_op jit(solution)/shard_map/ppermute | solution.py:271
  172.6 87.3 %collective-permute-start.51 = (bf16[2,160,640]{2,1,0:T(8,128)(2,1)}, bf16[2,160,640]{2,1,0:T(8,128)(2,1)}, u32[]{:S(2)}, u32[]{:S(2)}) collective-permute-start(bf16[2,160,640]{2,1,0:T(8,128)(2,1)} %pad_maximum_fusion.14), channel_id=1, source_target_pairs={{0,2},{1,3},{2,0},{3,1},{4,6},{5,7},{6,4},{7,5},{8,10},{9,11},{10,... | collective-permute-start | bytes 1228808 | tf_op jit(solution)/shard_map/ppermute | solution.py:271
  205.8 43.0 %collective-permute-start.29 = (bf16[160,640]{1,0:T(8,128)(2,1)}, bf16[160,640]{1,0:T(8,128)(2,1)}, u32[]{:S(2)}, u32[]{:S(2)}) collective-permute-start(bf16[160,640]{1,0:T(8,128)(2,1)} %bitcast.46.refs_0_), channel_id=1, source_target_pairs={{0,16},{16,0},{1,17},{17,1},{2,18},{18,2},{3,19},{19,3},{4,20},{20... | collective-permute-start | bytes 614408 | tf_op jit(solution)/shard_map/ppermute | solution.py:281
  206.3 44.0 %collective-permute-start.31 = (bf16[160,640]{1,0:T(8,128)(2,1)}, bf16[160,640]{1,0:T(8,128)(2,1)}, u32[]{:S(2)}, u32[]{:S(2)}) collective-permute-start(bf16[160,640]{1,0:T(8,128)(2,1)} %collective-permute-done.27.refs_2_), channel_id=1, source_target_pairs={{0,16},{16,0},{1,17},{17,1},{2,18},{18,2},{3,19},{19,3},{4,20},{20... | collective-permute-start | bytes 614408 | tf_op jit(solution)/shard_map/ppermute | solution.py:281
  207.8 43.0 %collective-permute-start.32 = (bf16[160,640]{1,0:T(8,128)(2,1)}, bf16[160,640]{1,0:T(8,128)(2,1)}, u32[]{:S(2)}, u32[]{:S(2)}) collective-permute-start(bf16[160,640]{1,0:T(8,128)(2,1)} %collective-permute-done.30.refs_5_), channel_id=1, source_target_pairs={{0,8},{8,0},{1,9},{9,1},{2,10},{10,2},{3,11},{11,3},{4,12},{12,4},... | collective-permute-start | bytes 614408 | tf_op jit(solution)/shard_map/ppermute | solution.py:281
  254.8 61.1 %collective-permute-start.33 = (bf16[1280,640]{1,0:T(8,128)(2,1)}, bf16[1280,640]{1,0:T(8,128)(2,1)}, u32[]{:S(2)}, u32[]{:S(2)}) collective-permute-start(bf16[1280,640]{1,0:T(8,128)(2,1)} %bitcast.564), channel_id=1, source_target_pairs={{0,4},{4,0},{1,5},{5,1},{2,6},{6,2},{3,7},{7,3},{8,12},{12,8},{9,1... | collective-permute-start | bytes 4915208 | tf_op jit(solution)/shard_map/ppermute | solution.py:33
  324.3 54.0 %collective-permute-start.34 = (bf16[512,1280]{1,0:T(8,128)(2,1)}, bf16[512,1280]{1,0:T(8,128)(2,1)}, u32[]{:S(2)}, u32[]{:S(2)}) collective-permute-start(bf16[512,1280]{1,0:T(8,128)(2,1)} %get-tuple-element.70), channel_id=1, source_target_pairs={{0,4},{4,0},{1,5},{5,1},{2,6},{6,2},{3,7},{7,3},{8,12},{12,8},{9,1... | collective-permute-start | bytes 3932168 | tf_op jit(solution)/shard_map/ppermute | solution.py:33
  422.7 65.7 %collective-permute-start.78 = (bf16[2,4,40,2560]{3,2,1,0:T(8,128)(2,1)}, bf16[2,4,40,2560]{3,2,1,0:T(8,128)(2,1)}, u32[]{:S(2)}, u32[]{:S(2)}) collective-permute-start(bf16[2,4,40,2560]{3,2,1,0:T(8,128)(2,1)} %dynamic-slice_bitcast_fusion), channel_id=1, source_target_pairs={{0,8},{8,0},{1,9},{9,1},{2,10},{10,2},{3,11},{11,3},{4,12},{12,4},... | collective-permute-start | bytes 4915208 | tf_op jit(solution)/shard_map/ppermute | solution.py:117
  425.7 64.8 %collective-permute-start.76 = (bf16[2,4,40,2560]{3,2,1,0:T(8,128)(2,1)}, bf16[2,4,40,2560]{3,2,1,0:T(8,128)(2,1)}, u32[]{:S(2)}, u32[]{:S(2)}) collective-permute-start(bf16[2,4,40,2560]{3,2,1,0:T(8,128)(2,1)} %dynamic-slice_bitcast_fusion.1), channel_id=1, source_target_pairs={{0,16},{16,0},{1,17},{17,1},{2,18},{18,2},{3,19},{19,3},{4,20},{20... | collective-permute-start | bytes 4915208 | tf_op jit(solution)/shard_map/ppermute | solution.py:117
  436.8 63.5 %collective-permute-start.71 = (bf16[2,4,160,640]{3,2,1,0:T(8,128)(2,1)}, bf16[2,4,160,640]{3,2,1,0:T(8,128)(2,1)}, u32[]{:S(2)}, u32[]{:S(2)}) collective-permute-start(bf16[2,4,160,640]{3,2,1,0:T(8,128)(2,1)} %dynamic-slice_bitcast_fusion.2), channel_id=1, source_target_pairs={{0,8},{8,0},{1,9},{9,1},{2,10},{10,2},{3,11},{11,3},{4,12},{12,4},... | collective-permute-start | bytes 4915208 | tf_op jit(solution)/shard_map/ppermute | solution.py:117
  438.8 72.9 %collective-permute-start.66 = (bf16[2,4,160,640]{3,2,1,0:T(8,128)(2,1)}, bf16[2,4,160,640]{3,2,1,0:T(8,128)(2,1)}, u32[]{:S(2)}, u32[]{:S(2)}) collective-permute-start(bf16[2,4,160,640]{3,2,1,0:T(8,128)(2,1)} %dynamic-slice_bitcast_fusion.3), channel_id=1, source_target_pairs={{0,16},{16,0},{1,17},{17,1},{2,18},{18,2},{3,19},{19,3},{4,20},{20... | collective-permute-start | bytes 4915208 | tf_op jit(solution)/shard_map/ppermute | solution.py:117
  500.3 47.3 %collective-permute-start.79 = (bf16[4,40,2560]{2,1,0:T(8,128)(2,1)S(1)}, bf16[4,40,2560]{2,1,0:T(8,128)(2,1)S(1)}, u32[]{:S(2)}, u32[]{:S(2)}) collective-permute-start(bf16[4,40,2560]{2,1,0:T(8,128)(2,1)S(1)} %dynamic-slice_bitcast_fusion.4), channel_id=1, source_target_pairs={{0,16},{16,0},{1,17},{17,1},{2,18},{18,2},{3,19},{19,3},{4,20},{20... | collective-permute-start | bytes 2457608 | tf_op jit(solution)/shard_map/ppermute | solution.py:117
  506.1 43.2 %collective-permute-start.77 = (bf16[4,40,2560]{2,1,0:T(8,128)(2,1)S(1)}, bf16[4,40,2560]{2,1,0:T(8,128)(2,1)S(1)}, u32[]{:S(2)}, u32[]{:S(2)}) collective-permute-start(bf16[4,40,2560]{2,1,0:T(8,128)(2,1)S(1)} %dynamic-slice_bitcast_fusion.5), channel_id=1, source_target_pairs={{0,8},{8,0},{1,9},{9,1},{2,10},{10,2},{3,11},{11,3},{4,12},{12,4},... | collective-permute-start | bytes 2457608 | tf_op jit(solution)/shard_map/ppermute | solution.py:117
  507.6 41.8 %collective-permute-start.72 = (bf16[4,160,640]{2,1,0:T(8,128)(2,1)S(1)}, bf16[4,160,640]{2,1,0:T(8,128)(2,1)S(1)}, u32[]{:S(2)}, u32[]{:S(2)}) collective-permute-start(bf16[4,160,640]{2,1,0:T(8,128)(2,1)S(1)} %dynamic-slice_bitcast_fusion.6), channel_id=1, source_target_pairs={{0,16},{16,0},{1,17},{17,1},{2,18},{18,2},{3,19},{19,3},{4,20},{20... | collective-permute-start | bytes 2457608 | tf_op jit(solution)/shard_map/ppermute | solution.py:117
  591.0 91.4 %collective-permute-start.123 = (bf16[40,2560]{1,0:T(8,128)(2,1)}, bf16[40,2560]{1,0:T(8,128)(2,1)}, u32[]{:S(2)}, u32[]{:S(2)}) collective-permute-start(bf16[40,2560]{1,0:T(8,128)(2,1)} %get-tuple-element.119), channel_id=1, source_target_pairs={{0,1},{1,2},{2,3},{3,0},{4,5},{5,6},{6,7},{7,4},{8,9},{9,10},{10,1... | collective-permute-start | bytes 614408 | tf_op jit(solution)/shard_map/ppermute | solution.py:117
  594.8 89.1 %collective-permute-start.124 = (bf16[40,2560]{1,0:T(8,128)(2,1)}, bf16[40,2560]{1,0:T(8,128)(2,1)}, u32[]{:S(2)}, u32[]{:S(2)}) collective-permute-start(bf16[40,2560]{1,0:T(8,128)(2,1)} %get-tuple-element.121), channel_id=1, source_target_pairs={{0,2},{1,3},{2,0},{3,1},{4,6},{5,7},{6,4},{7,5},{8,10},{9,11},{10,... | collective-permute-start | bytes 614408 | tf_op jit(solution)/shard_map/ppermute | solution.py:117
  598.8 85.1 %collective-permute-start.125 = (bf16[40,2560]{1,0:T(8,128)(2,1)}, bf16[40,2560]{1,0:T(8,128)(2,1)}, u32[]{:S(2)}, u32[]{:S(2)}) collective-permute-start(bf16[40,2560]{1,0:T(8,128)(2,1)} %get-tuple-element.120), channel_id=1, source_target_pairs={{0,3},{1,0},{2,1},{3,2},{4,7},{5,4},{6,5},{7,6},{8,11},{9,8},{10,9... | collective-permute-start | bytes 614408 | tf_op jit(solution)/shard_map/ppermute | solution.py:117
  609.7 74.2 %collective-permute-start.120 = (bf16[40,2560]{1,0:T(8,128)(2,1)}, bf16[40,2560]{1,0:T(8,128)(2,1)}, u32[]{:S(2)}, u32[]{:S(2)}) collective-permute-start(bf16[40,2560]{1,0:T(8,128)(2,1)} %get-tuple-element.122), channel_id=1, source_target_pairs={{0,1},{1,2},{2,3},{3,0},{4,5},{5,6},{6,7},{7,4},{8,9},{9,10},{10,1... | collective-permute-start | bytes 614408 | tf_op jit(solution)/shard_map/ppermute | solution.py:117
  613.3 70.6 %collective-permute-start.121 = (bf16[40,2560]{1,0:T(8,128)(2,1)}, bf16[40,2560]{1,0:T(8,128)(2,1)}, u32[]{:S(2)}, u32[]{:S(2)}) collective-permute-start(bf16[40,2560]{1,0:T(8,128)(2,1)} %get-tuple-element.124), channel_id=1, source_target_pairs={{0,2},{1,3},{2,0},{3,1},{4,6},{5,7},{6,4},{7,5},{8,10},{9,11},{10,... | collective-permute-start | bytes 614408 | tf_op jit(solution)/shard_map/ppermute | solution.py:117
  697.6 46.5 %collective-permute-start.96 = (bf16[2,4,40,1152]{3,2,1,0:T(8,128)(2,1)}, bf16[2,4,40,1152]{3,2,1,0:T(8,128)(2,1)}, u32[]{:S(2)}, u32[]{:S(2)}) collective-permute-start(bf16[2,4,40,1152]{3,2,1,0:T(8,128)(2,1)} %dynamic-slice_bitcast_fusion.8), channel_id=1, source_target_pairs={{0,8},{8,0},{1,9},{9,1},{2,10},{10,2},{3,11},{11,3},{4,12},{12,4},... | collective-permute-start | bytes 2211848 | tf_op jit(solution)/shard_map/ppermute | solution.py:117
  (195 other events, 3188.3 us)
